TPU v7x, 512 devices: a whole 4x4x16 slice. The times are simulated.
512 devices in a mesh: ctx: 128 (over x, y, z_hi, core), tp: 4 (over z_lo).
Axes of the slice: x: 4, y: 4, z: 16 (z_hi: 4, z_lo: 4; z = z_hi * 4 + z_lo), core: 2. Of those that a mesh axis runs over, the one named last changes fastest.
Arguments:
- x_gate: bfloat16 [16384, 2048], P('ctx', 'tp'), may hold values from -6 to 6
- x_post: bfloat16 [16384, 2048], P('ctx', 'tp'), may hold values from -6 to 6
- values: bfloat16 [16384, 2048], P('ctx', 'tp'), may hold values from -6 to 6
- decay: float32 [2, 2048, 16], P(None, 'tp'), may hold values from 1.5258789e-05 to 0.05
- residue: float32 [2, 2048, 16], P(None, 'tp'), may hold values from -4 to 4
- w_out: bfloat16 [2048, 2048], P(('tp', 'ctx')), may hold values from -0.125 to 0.125
Outputs:
- projected: bfloat16 [16384, 2048], P('ctx', 'tp')
All inputs are finite; a program needn't handle non-finite values.
Results may differ from a plain program's by a relative error of at most 0.015.
Values may be sent and summed in bfloat16 or wider, within the bound.
A program may use at most 128 MiB of HBM per device.

v0:
```python
import math

import jax
import jax.numpy as jnp
from jax import lax
from jax.sharding import PartitionSpec as P

HIGHEST = lax.Precision.HIGHEST


def partner(value, axis, bit):
    mask = 2**bit
    pairs = [(source, source ^ mask) for source in range(lax.axis_size(axis))]
    return lax.ppermute(value, axis, pairs)


def radices(length_all):
    last_radix = min(128, length_all // 4)
    first_radix = min(32, length_all // last_radix)
    return (first_radix, length_all // (first_radix * last_radix), last_radix)


def rotation(row_count, col_count, modulus):
    product = (
        lax.broadcasted_iota(jnp.int32, (row_count, col_count), 0)
        * lax.broadcasted_iota(jnp.int32, (row_count, col_count), 1)
        % modulus
    )
    angle = product.astype(jnp.float32) * (2.0 * math.pi / modulus)
    return (jnp.cos(angle), -jnp.sin(angle))


def tables(radix_sizes):
    first_radix, mid_radix, last_radix = radix_sizes
    length_all = first_radix * mid_radix * last_radix
    outer_real, outer_imag = rotation(first_radix, first_radix, first_radix)
    mid_real, mid_imag = rotation(mid_radix, mid_radix, mid_radix)
    last_real, last_imag = rotation(last_radix, last_radix, last_radix)
    twist_real, twist_imag = rotation(first_radix, mid_radix * last_radix, length_all)
    twist_real = twist_real.reshape(first_radix, mid_radix, last_radix)
    twist_imag = twist_imag.reshape(first_radix, mid_radix, last_radix)
    inner_real, inner_imag = rotation(mid_radix, last_radix, mid_radix * last_radix)
    return (
        outer_real,
        outer_imag,
        mid_real,
        mid_imag,
        last_real,
        last_imag,
        twist_real,
        twist_imag,
        inner_real,
        inner_imag,
    )


def apply_matrix(pattern, real_part, imag_part, matrix_real, matrix_imag):
    out_real = jnp.einsum(pattern, real_part, matrix_real, precision=HIGHEST) - jnp.einsum(
        pattern, imag_part, matrix_imag, precision=HIGHEST
    )
    out_imag = jnp.einsum(pattern, real_part, matrix_imag, precision=HIGHEST) + jnp.einsum(
        pattern, imag_part, matrix_real, precision=HIGHEST
    )
    return (out_real, out_imag)


def complex_times(left_real, left_imag, right_real, right_imag):
    return (
        left_real * right_real - left_imag * right_imag,
        left_real * right_imag + left_imag * right_real,
    )


def forward(real_part, imag_part, table_set, radix_sizes):
    first_radix, mid_radix, last_radix = radix_sizes
    half_first = first_radix // 2
    batch_rows = real_part.shape[0]
    (
        outer_real,
        outer_imag,
        mid_real,
        mid_imag,
        last_real,
        last_imag,
        twist_real,
        twist_imag,
        inner_real,
        inner_imag,
    ) = table_set
    real_part = real_part.reshape(batch_rows, half_first, mid_radix, last_radix)
    imag_part = imag_part.reshape(batch_rows, half_first, mid_radix, last_radix)
    real_part, imag_part = apply_matrix(
        "banm,ak->bknm", real_part, imag_part, outer_real[:half_first], outer_imag[:half_first]
    )
    real_part, imag_part = complex_times(real_part, imag_part, twist_real, twist_imag)
    real_part, imag_part = apply_matrix("bknm,nj->bkjm", real_part, imag_part, mid_real, mid_imag)
    real_part, imag_part = complex_times(real_part, imag_part, inner_real, inner_imag)
    return apply_matrix("bkjm,mq->bkjq", real_part, imag_part, last_real, last_imag)


def inverse(real_part, imag_part, table_set, radix_sizes):
    first_radix, mid_radix, last_radix = radix_sizes
    half_first = first_radix // 2
    batch_rows = real_part.shape[0]
    (
        outer_real,
        outer_imag,
        mid_real,
        mid_imag,
        last_real,
        last_imag,
        twist_real,
        twist_imag,
        inner_real,
        inner_imag,
    ) = table_set
    real_part, imag_part = apply_matrix(
        "bkjq,mq->bkjm", real_part, imag_part, last_real / last_radix, -last_imag / last_radix
    )
    real_part, imag_part = complex_times(real_part, imag_part, inner_real, -inner_imag)
    real_part, imag_part = apply_matrix(
        "bkjm,nj->bknm", real_part, imag_part, mid_real / mid_radix, -mid_imag / mid_radix
    )
    real_part, imag_part = complex_times(real_part, imag_part, twist_real, -twist_imag)
    matrix_real = outer_real[:half_first] / first_radix
    matrix_imag = -outer_imag[:half_first] / first_radix
    out_real, out_imag = apply_matrix(
        "bknm,ak->banm", real_part, imag_part, matrix_real, matrix_imag
    )
    return (out_real.reshape(batch_rows, -1), out_imag.reshape(batch_rows, -1))


def spectrum(decay_rows, residue_rows, radix_sizes, seq_length):
    first_radix, mid_radix, last_radix = radix_sizes
    length_all = first_radix * mid_radix * last_radix
    poles = decay_rows.shape[1]
    shape_all = (first_radix, mid_radix, last_radix)
    frequency = (
        lax.broadcasted_iota(jnp.int32, shape_all, 0)
        + first_radix * lax.broadcasted_iota(jnp.int32, shape_all, 1)
        + first_radix * mid_radix * lax.broadcasted_iota(jnp.int32, shape_all, 2)
    )
    half_angle = frequency.astype(jnp.float32) * (math.pi / length_all)
    sin_half = jnp.sin(half_angle)
    sin_full = jnp.sin(2.0 * half_angle)
    parity_sign = (1 - 2 * (frequency % 2)).astype(jnp.float32)

    def add_pole(pole_index, running):
        run_real, run_imag = running
        rate_col = lax.dynamic_slice_in_dim(decay_rows, pole_index, 1, 1).reshape(-1, 1, 1, 1)
        weight = lax.dynamic_slice_in_dim(residue_rows, pole_index, 1, 1).reshape(
            -1, 1, 1, 1
        ) * jnp.sqrt(2.0 * rate_col / poles)
        retained = jnp.exp(-rate_col)
        den_real = -jnp.expm1(-rate_col) + 2.0 * retained * sin_half * sin_half
        den_imag = retained * sin_full
        pole_scale = (
            weight
            * (1.0 - jnp.exp(-rate_col * seq_length) * parity_sign)
            / (den_real * den_real + den_imag * den_imag)
        )
        return (run_real + pole_scale * den_real, run_imag - pole_scale * den_imag)

    zeros_all = jnp.zeros((decay_rows.shape[0],) + shape_all, jnp.float32)
    return lax.fori_loop(0, poles, add_pole, (zeros_all, zeros_all))


def local(x_gate, x_post, values, decay, residue, w_out):
    tok_rows, block_width = x_gate.shape
    ctx_count = lax.axis_size("ctx")
    tp_count = lax.axis_size("tp")
    chan_group = block_width // ctx_count
    seq_length = tok_rows * ctx_count
    radix_sizes = radices(2 * seq_length)
    table_set = tables(radix_sizes)
    first_row = lax.axis_index("ctx") * chan_group
    own_rate = lax.dynamic_slice_in_dim(decay, first_row, chan_group, 1)
    own_residue = lax.dynamic_slice_in_dim(residue, first_row, chan_group, 1)
    own_spec = [
        spectrum(own_rate[filter_index], own_residue[filter_index], radix_sizes, seq_length)
        for filter_index in range(2)
    ]
    forward_rows = [x_gate, values] + [x_post]
    row_count = len(forward_rows)
    base_rows = jnp.stack(forward_rows)
    copied = base_rows
    for bit_index in range(tp_count.bit_length() - 1):
        copied = partner(copied, "tp", bit_index)
    sent_rows = jnp.concatenate([base_rows, copied[:, :, ::-1]], axis=0)
    received = lax.all_to_all(
        jnp.swapaxes(sent_rows, 1, 2), "ctx", split_axis=1, concat_axis=2, tiled=True
    )
    gate_fwd = received[0].astype(jnp.float32)
    value_fwd = received[1].astype(jnp.float32)
    mirrored = received[row_count:, :, ::-1].astype(jnp.float32)
    spec_real, spec_imag = forward(value_fwd, mirrored[1], table_set, radix_sizes)
    spec_real, spec_imag = complex_times(spec_real, spec_imag, own_spec[0][0], own_spec[0][1])
    along_fwd, along_rev = inverse(spec_real, spec_imag, table_set, radix_sizes)
    spec_real, spec_imag = forward(
        gate_fwd * along_fwd, mirrored[0] * along_rev, table_set, radix_sizes
    )
    spec_real, spec_imag = complex_times(spec_real, spec_imag, own_spec[1][0], own_spec[1][1])
    sum_fwd, sum_rev = inverse(spec_real, spec_imag, table_set, radix_sizes)
    sum_fwd = received[2].astype(jnp.float32) * sum_fwd
    sum_rev = mirrored[2] * sum_rev
    results = jnp.stack([sum_fwd, sum_rev[:, ::-1]])
    returned = lax.all_to_all(
        results.astype(jnp.bfloat16), "ctx", split_axis=2, concat_axis=1, tiled=True
    ).astype(results.dtype)
    flipped = returned[1, ::-1, :]
    for bit_index in range(tp_count.bit_length() - 1):
        flipped = partner(flipped.astype(jnp.bfloat16), "tp", bit_index).astype(flipped.dtype)
    total_rows = returned[0] + flipped
    total_rows = total_rows.T
    mixed_rows = total_rows.astype(jnp.bfloat16)
    whole_rows = lax.all_gather(mixed_rows, "tp", axis=1, tiled=True)
    projected = lax.dot_general(
        whole_rows,
        lax.all_gather(w_out, "ctx", axis=0, tiled=True),
        (((1,), (1,)), ((), ())),
        preferred_element_type=jnp.float32,
    )
    return projected.astype(jnp.bfloat16)


def solution(mesh):
    in_specs = (
        P("ctx", "tp"),
        P("ctx", "tp"),
        P("ctx", "tp"),
        P(None, "tp", None),
        P(None, "tp", None),
        P(("tp", "ctx"), None),
    )
    out_specs = P("ctx", "tp")
    return jax.shard_map(local, mesh=mesh, in_specs=in_specs, out_specs=out_specs, check_vma=False)
```

profile of v0, /device:TPU:8, one launch (start us, length us, event | category | flops | bytes accessed | tf_op | source)
XLA Modules:
  0.0 463.1 jit_solution(8787440911086789286)
XLA Ops:
  7.6 3.8 collective-permute-start
  11.5 1.4 dynamic-slice_bitcast_fusion
  13.0 7.6 %collective-permute-done = bf16[3,128,512]{2,1,0:T(8,128)(2,1)S(1)} collective-permute-done((bf16[3,128,512]{2,1,0:T(8,128)(2,1)S(1)}, bf16[3,128,512]{2,1,0:T(8,128)(2,1)S(1)}, u32[]{:S(2)}, u32[]{:S(2)}) %collective-permute-start) | collective-permute-done | bytes 393248 | tf_op jit(solution)/shard_map/ppermute | solution.py:14
  20.5 5.2 %collective-permute-start.1 = (bf16[3,128,512]{2,1,0:T(8,128)(2,1)S(1)}, bf16[3,128,512]{2,1,0:T(8,128)(2,1)S(1)}, u32[]{:S(2)}, u32[]{:S(2)}) collective-permute-start(bf16[3,128,512]{2,1,0:T(8,128)(2,1)S(1)} %collective-permute-done), channel_id=1, source_target_pairs={{0,2},{1,3},{2,0},{3,1},{4,6},{5,7},{6,4},{7,5},{8,10},{9,11},{10,... | collective-permute-start | bytes 1179656 | tf_op jit(solution)/shard_map/ppermute | solution.py:14
  25.7 27.2 %while.42 = (s32[]{:T(128)}, f32[4,32,8,128]{3,2,1,0:T(8,128)S(1)}, f32[4,32,8,128]{3,2,1,0:T(8,128)S(1)}, f32[4,16]{0,1:T(8,128)S(1)}, f32[4,16]{0,1:T(8,128)S(...) while((s32[]{:T(128)}, f32[4,32,8,128]{3,2,1,0:T(8,128)S(1)}, ...), condition=%wide.region_1.2_spmd.clone.clone.clone.clone, body=%wide.region_0.1_spmd.clone.clone.clone.clone.sunk | while | flops 2916379 | bytes 2885019 | solution.py:165
  53.0 1.2 rev.12
  55.3 1.5 copy.297
  56.7 20.0 %all-to-all-start = ((bf16[6,512,128]{2,0,1:T(8,128)(2,1)}), bf16[6,512,128]{2,0,1:T(8,128)(2,1)S(1)}, u32[]{:S(2)}, u32[]{:S(2)}) async-start(bf16[6,512,128]{2,0,1:T(8,128)(2,1)} %copy.297), calls=%async_computation | async-start | bytes 2097152 | tf_op jit(solution)/shard_map/all_to_all | solution.py:190
  76.7 66.6 %while.43 = (s32[]{:T(128)}, f32[4,32,8,128]{3,2,1,0:T(8,128)S(1)}, f32[4,32,8,128]{3,2,1,0:T(8,128)S(1)}, f32[4,16]{0,1:T(8,128)}, f32[4,16]{0,1:T(8,128)}, /*i...) while((s32[]{:T(128)}, f32[4,32,8,128]{3,2,1,0:T(8,128)S(1)}, ...), condition=%wide.region_3.4_spmd.clone.clone.clone.clone, body=%wide.region_2.3_spmd.clone.clone.clone.clone.sunk | while | flops 2916379 | bytes 2885019 | solution.py:165
  79.7 1.2 fusion.445
  83.8 1.2 fusion.445
  108.8 1.2 fusion.445
  113.0 1.2 fusion.445
  148.5 1.6 slice.102
  150.1 56.7 %slice.103 = bf16[1,4,16384]{2,1,0:T(4,128)(2,1)} reverse(bf16[1,4,16384]{2,1,0:T(4,128)(2,1)} %slice.102), dimensions={2} | reverse | bytes 262144 | tf_op jit(solution)/shard_map/slice | solution.py:196
  219.7 11.9 %fusion.75 = f32[8,4,32,128]{3,0,2,1:T(8,128)S(1)} fusion(f32[4,32,8,128]{3,2,1,0:T(8,128)S(1)} %convolution_add_fusion.7, f32[4,32,8,128]{3,2,1,0:T(8,128)S(1)} %convolution_subtract_fusion.7, f32[8,128]{1,0:T(8,128)S(1)} %fusion.235, f32[8,128]{1,0:T(8,128)S(1)} %get-tuple-element.800), kind=kOutput, calls=%fused_computation.160 | convolution fusion | flops 12977088 | bytes 1581056 | tf_op jit(solution)/shard_map/bkjm,nj->bknm/dot_general | solution.py:58
  236.0 1.5 fusion.169
  238.3 43.1 %rev.13 = bf16[3,4,16384]{2,1,0:T(4,128)(2,1)} reverse(bf16[3,4,16384]{2,1,0:T(4,128)(2,1)S(1)} %slice.107), dimensions={2} | reverse | bytes 786432 | tf_op jit(solution)/shard_map/rev | solution.py:195
  282.6 1.4 fusion.35
  301.2 11.5 %rev.14 = bf16[4,16384]{1,0:T(4,128)(2,1)S(1)} reverse(bf16[4,16384]{1,0:T(4,128)(2,1)S(1)} %bitcast_multiply_fusion), dimensions={1} | reverse | bytes 262144 | tf_op jit(solution)/shard_map/rev | solution.py:206
  313.5 13.1 %copy.344 = bf16[2,4,16384]{1,0,2:T(2,128)(2,1)} copy(bf16[2,4,16384]{2,0,1:T(2,128)(2,1)S(1)} %pad_maximum_fusion.1) | data formatting | bytes 524288 | tf_op jit(solution)/shard_map/stack | solution.py:206
  326.5 16.2 %reshape.346 = bf16[128,2,512]{2,1,0:T(2,128)(2,1)S(1)} reshape(bf16[16384,2,4]{2,1,0:T(2,128)(2,1)} %bitcast.313) | data formatting | bytes 524288
  342.7 39.2 %all_to_all.24 = bf16[128,2,512]{2,1,0:T(2,128)(2,1)S(1)} all-to-all(bf16[128,2,512]{2,1,0:T(2,128)(2,1)S(1)} %reshape.346), channel_id=1, replica_groups=mesh['ctx'=128,'tp'=4] {'ctx'}, dimensions={0} | all-to-all | bytes 524288 | tf_op jit(solution)/shard_map/all_to_all | solution.py:207
  382.0 19.1 %reshape.347 = bf16[16384,2,4]{2,1,0:T(2,128)(2,1)} reshape(bf16[128,2,512]{2,1,0:T(2,128)(2,1)S(1)} %all_to_all.24) | data formatting | bytes 524288
  401.1 16.3 %copy.345 = f32[2,4,128,128]{3,1,2,0:T(4,128)S(1)} copy(bf16[2,4,128,128]{1,0,3,2:T(2,128)(2,1)} %bitcast.314) | data formatting | bytes 786432 | tf_op jit(solution)/shard_map/convert_element_type | solution.py:209
  417.6 6.6 %collective-permute-start.2 = (bf16[512,128]{1,0:T(8,128)(2,1)S(1)}, bf16[512,128]{1,0:T(8,128)(2,1)S(1)}, u32[]{:S(2)}, u32[]{:S(2)}) collective-permute-start(bf16[512,128]{1,0:T(8,128)(2,1)S(1)} %bitcast.336), channel_id=1, source_target_pairs={{0,1},{1,0},{2,3},{3,2},{4,5},{5,4},{6,7},{7,6},{8,9},{9,8},{10,11... | collective-permute-start | bytes 393224 | tf_op jit(solution)/shard_map/ppermute | solution.py:14
  424.2 3.8 collective-permute-done.2
  428.0 4.1 collective-permute-start.3
  432.1 2.5 reshape.327
  434.7 3.9 collective-permute-done.3
  438.6 15.8 %all_gather.6 = bf16[128,2048]{0,1:T(8,128)(2,1)S(1)} all-gather(bf16[128,512]{0,1:T(8,128)(2,1)S(1)} %fusion.81), channel_id=1, replica_groups=mesh['ctx'=128,'tp'=4] {'tp'}, dimensions={1}, use_global_device_ids=true | all-gather | bytes 655360 | tf_op jit(solution)/shard_map/all_gather | solution.py:216
  454.4 1.5 convolution_convert_fusion
  (295 shorter events, 131.8 us)
Async XLA Ops:
  6.5 425.6 %all-gather.3.cloned.1.call-start = ((), (), s32[]{:S(2)}) async-start(), calls=%async_computation.2 | async-start | bytes 2113536 | tf_op jit(solution)/shard_map/all_gather | solution.py:219
  7.6 12.9 %collective-permute-start = (bf16[3,128,512]{2,1,0:T(8,128)(2,1)S(1)}, bf16[3,128,512]{2,1,0:T(8,128)(2,1)S(1)}, u32[]{:S(2)}, u32[]{:S(2)}) collective-permute-start(bf16[3,128,512]{2,1,0:T(8,128)(2,1)S(1)} %pad_maximum_fusion), channel_id=1, source_target_pairs={{0,1},{1,0},{2,3},{3,2},{4,5},{5,4},{6,7},{7,6},{8,9},{9,8},{10,11... | collective-permute-start | bytes 1179656 | tf_op jit(solution)/shard_map/ppermute | solution.py:14
  20.5 32.4 %collective-permute-start.1 = (bf16[3,128,512]{2,1,0:T(8,128)(2,1)S(1)}, bf16[3,128,512]{2,1,0:T(8,128)(2,1)S(1)}, u32[]{:S(2)}, u32[]{:S(2)}) collective-permute-start(bf16[3,128,512]{2,1,0:T(8,128)(2,1)S(1)} %collective-permute-done), channel_id=1, source_target_pairs={{0,2},{1,3},{2,0},{3,1},{4,6},{5,7},{6,4},{7,5},{8,10},{9,11},{10,... | collective-permute-start | bytes 1179656 | tf_op jit(solution)/shard_map/ppermute | solution.py:14
  25.7 28.5 %copy-start.10 = (bf16[128,512]{1,0:T(8,128)(2,1)S(1)}, bf16[128,512]{1,0:T(8,128)(2,1)}, u32[]{:S(2)}) copy-start(bf16[128,512]{1,0:T(8,128)(2,1)} %param.11) | copy-start | bytes 393220
  25.7 28.5 %copy-start.11 = (bf16[128,512]{1,0:T(8,128)(2,1)S(1)}, bf16[128,512]{1,0:T(8,128)(2,1)}, u32[]{:S(2)}) copy-start(bf16[128,512]{1,0:T(8,128)(2,1)} %param.12) | copy-start | bytes 393220
  56.7 88.8 %all-to-all-start = ((bf16[6,512,128]{2,0,1:T(8,128)(2,1)}), bf16[6,512,128]{2,0,1:T(8,128)(2,1)S(1)}, u32[]{:S(2)}, u32[]{:S(2)}) async-start(bf16[6,512,128]{2,0,1:T(8,128)(2,1)} %copy.297), calls=%async_computation | async-start | bytes 2097152 | tf_op jit(solution)/shard_map/all_to_all | solution.py:190
  145.8 0.9 copy-start
  218.2 13.4 %copy-start.1 = (bf16[6,128,4,128]{3,1,2,0:T(8,128)(2,1)S(1)}, bf16[6,128,4,128]{3,1,2,0:T(8,128)(2,1)}, u32[]{:S(2)}) copy-start(bf16[6,128,4,128]{3,1,2,0:T(8,128)(2,1)} %copy-done) | copy-start | bytes 2359300
  219.7 13.4 %copy-start.4 = (f32[32,8,128]{2,1,0:T(8,128)S(1)}, f32[32,8,128]{2,1,0:T(8,128)}, u32[]{:S(2)}) copy-start(f32[32,8,128]{2,1,0:T(8,128)} %copy.316) | copy-start | bytes 393220
  219.7 13.4 %copy-start.6 = (f32[32,8,128]{2,1,0:T(8,128)S(1)}, f32[32,8,128]{2,1,0:T(8,128)}, u32[]{:S(2)}) copy-start(f32[32,8,128]{2,1,0:T(8,128)} %copy.317) | copy-start | bytes 393220
  233.1 2.5 copy-start.9
  233.9 4.3 copy-start.3
  281.4 2.6 copy-start.2
  296.6 1.3 copy-start.5
  296.6 1.3 copy-start.7
  299.1 1.6 copy-start.8
  417.6 10.4 %collective-permute-start.2 = (bf16[512,128]{1,0:T(8,128)(2,1)S(1)}, bf16[512,128]{1,0:T(8,128)(2,1)S(1)}, u32[]{:S(2)}, u32[]{:S(2)}) collective-permute-start(bf16[512,128]{1,0:T(8,128)(2,1)S(1)} %bitcast.336), channel_id=1, source_target_pairs={{0,1},{1,0},{2,3},{3,2},{4,5},{5,4},{6,7},{7,6},{8,9},{9,8},{10,11... | collective-permute-start | bytes 393224 | tf_op jit(solution)/shard_map/ppermute | solution.py:14
  428.0 10.6 %collective-permute-start.3 = (bf16[512,128]{1,0:T(8,128)(2,1)S(1)}, bf16[512,128]{1,0:T(8,128)(2,1)S(1)}, u32[]{:S(2)}, u32[]{:S(2)}) collective-permute-start(bf16[512,128]{1,0:T(8,128)(2,1)S(1)} %collective-permute-done.2), channel_id=1, source_target_pairs={{0,2},{1,3},{2,0},{3,1},{4,6},{5,7},{6,4},{7,5},{8,10},{9,11},{10,... | collective-permute-start | bytes 393224 | tf_op jit(solution)/shard_map/ppermute | solution.py:14
Sparse Core Ops, SparseCore 0:
  11.8 134.8 all-gather.2
where the time goes:
time: 472 us; the launch traced here: 463 us
  local copies, waits for them, and re-layouts  189 us (40%)
  other arithmetic  98.2 us (21%)
  blocking collectives  55 us (12%)
  matrix products  49.5 us (10%)
  starting transfers between devices  39.7 us (8%)
  waiting for transfers between devices  15.3 us (3%)
  between operations  14.6 us (3%)
    slice x2, local copies, waits for them, and re-layouts, local(): mirrored[1]  58.3 us
    rev x1, local copies, waits for them, and re-layouts, local(): mirrored = received[row_count:, :, ::-1].astype(jnp.float32)  43.1 us
    unnamed x30, local copies, waits for them, and re-layouts  39.7 us
    all_to_all x1, blocking collectives, local(): lax.all_to_all(results.astype(jnp.bfloat16), 'ctx', split_axis=2, concat_...  39.2 us
    sin x32, other arithmetic, spectrum(): sin_full = jnp.sin(2.0 * half_angle)  29.9 us
    sub x32, other arithmetic, add_pole(): return (run_real + pole_scale * den_real, run_imag - pole_scale * den_imag)  28 us
    all_to_all x1, starting transfers between devices, local(): lax.all_to_all(jnp.swapaxes(sent_rows, 1, 2), 'ctx', split_axis=1, concat...  20 us
    ppermute x4, starting transfers between devices, partner(): return lax.ppermute(value, axis, pairs)  19.7 us
  transfers between devices with their start and end apart: 6, of which 3 were waited for; matrix products, arithmetic and copies ran while one was open for 72% of the time, Pallas kernels for 0%

commit v1 on v0

v1 whole, which is shorter than its diff:
```python
import jax
import jax.numpy as jnp
from jax import lax
from jax.experimental import pallas as pl
from jax.experimental.pallas import tpu as pltpu
from jax.sharding import PartitionSpec as P

MESH = pl.DeviceIdType.MESH
F32 = jnp.float32
BF16 = jnp.bfloat16

POLES = 16
CHUNK = 128
STEPS = 16
SUBS = 8
LANES = 128
TILES = 4
GROUP = 8
PLANES = 16
TP = 4
WIDTH = TILES * LANES


def mixer_kernel(
    gate_hbm,
    post_hbm,
    vals_hbm,
    decay_hbm,
    residue_hbm,
    w_hbm,
    out_ref,
    gate_s,
    post_s,
    vals_s,
    decay_s,
    residue_s,
    w_s,
    params,
    flipped,
    rate,
    weight,
    v4,
    g4,
    p4,
    y4,
    u4,
    finals,
    inits,
    corr,
    state_out,
    state_in,
    total_out,
    total_in,
    carry_out,
    carry_in,
    w_pair,
    w_chip,
    w_planes,
    w_rows,
    w_full,
    mix_f32,
    mix,
    acc,
    load_sem,
    par_send,
    par_recv,
    st_send,
    st_recv,
    tot_send,
    tot_recv,
    car_send,
    car_recv,
    w_send,
    w_recv,
    mix_send,
    mix_recv,
):
    ctx = lax.axis_index("ctx")
    tp = lax.axis_index("tp")
    plane = ctx // GROUP
    slot = lax.rem(ctx, GROUP)
    z_hi = slot // 2
    core = lax.rem(slot, 2)
    my_dir = slot // TILES
    my_tile = lax.rem(slot, TILES)

    loads = [
        pltpu.make_async_copy(src, dst, load_sem.at[index])
        for index, (src, dst) in enumerate(
            [
                (decay_hbm, decay_s),
                (residue_hbm, residue_s),
                (vals_hbm, vals_s),
                (w_hbm, w_s),
                (gate_hbm, gate_s),
                (post_hbm, post_s),
            ]
        )
    ]
    for load in loads:
        load.start()

    barrier = pltpu.get_barrier_semaphore()
    for offset in range(1, TP):
        pl.semaphore_signal(
            barrier, inc=1, device_id={"tp": lax.rem(tp + offset, TP)}, device_id_type=MESH
        )
    for offset in range(1, GROUP):
        peer = plane * GROUP + lax.rem(slot + offset, GROUP)
        pl.semaphore_signal(barrier, inc=1, device_id={"ctx": peer}, device_id_type=MESH)
    for offset in range(1, PLANES):
        peer = lax.rem(plane + offset, PLANES) * GROUP + slot
        pl.semaphore_signal(barrier, inc=1, device_id={"ctx": peer}, device_id_type=MESH)

    row_id = lax.broadcasted_iota(jnp.int32, (LANES, 2 * LANES), 0)
    col_id = lax.broadcasted_iota(jnp.int32, (LANES, 2 * LANES), 1)
    picks = ((row_id == col_id) | (row_id + col_id == 2 * LANES - 1)).astype(F32)
    loads[0].wait()
    loads[1].wait()
    for filt in range(2):
        for which, source in enumerate((decay_s, residue_s)):
            for tile in range(TILES):
                both = lax.dot_general(
                    source[filt, tile * LANES : (tile + 1) * LANES, :],
                    picks,
                    (((0,), (0,)), ((), ())),
                    precision=lax.Precision.HIGHEST,
                    preferred_element_type=F32,
                )
                params[filt, 0, which, tile] = both[:, :LANES]
                flipped[filt, which, TILES - 1 - tile] = both[:, LANES:]
    loads[3].wait()
    w_pair[core] = w_s[...].astype(F32)

    pl.semaphore_wait(barrier, (TP - 1) + (GROUP - 1) + (PLANES - 1))

    par_copies = []
    for filt in range(2):
        copy = pltpu.make_async_remote_copy(
            src_ref=flipped.at[filt],
            dst_ref=params.at[filt, 1],
            send_sem=par_send.at[filt],
            recv_sem=par_recv.at[filt],
            device_id={"tp": TP - 1 - tp},
            device_id_type=MESH,
        )
        copy.start()
        par_copies.append(copy)
    w_core = pltpu.make_async_remote_copy(
        src_ref=w_pair.at[core],
        dst_ref=w_pair.at[core],
        send_sem=w_send.at[0],
        recv_sem=w_recv.at[0],
        device_id={"ctx": ctx + 1 - 2 * core},
        device_id_type=MESH,
    )
    w_core.start()

    def derive(filt, side):
        for tile in range(TILES):
            decay = params[filt, side, 0, tile]
            rate[filt, side, tile] = jnp.exp(-decay)
            weight[filt, side, tile] = params[filt, side, 1, tile] * jnp.sqrt(
                2.0 * decay / POLES
            )

    def row8(ref, filt, side, tile, pole):
        return jnp.broadcast_to(ref[filt, side, tile, pole : pole + 1, :], (SUBS, LANES))

    def step_order(side):
        return range(STEPS) if side == 0 else range(STEPS - 1, -1, -1)

    def sub_order(side):
        return range(SUBS) if side == 0 else range(SUBS - 1, -1, -1)

    def picked(ref, tile, step):
        return ref[tile, pl.ds(step, SUBS, stride=STEPS), :]

    def chunk_states(filt, side, tile, xs):
        order = step_order(side)
        for pole in range(POLES):
            a = row8(rate, filt, side, tile, pole)
            state = xs[order[0]]
            for step in order[1:]:
                state = a * state + xs[step]
            finals[side, pole * SUBS : (pole + 1) * SUBS, :] = state
        a_sub = jnp.exp(-float(STEPS) * params[filt, side, 0, tile])
        running = [jnp.zeros((SUBS, LANES), F32) for _ in range(2)]
        for sub in sub_order(side):
            for half in range(2):
                rows = pl.ds(half * 64 + sub, 8, stride=SUBS)
                inits[side, tile, rows, :] = running[half]
                running[half] = (
                    a_sub[half * 8 : half * 8 + 8] * running[half] + finals[side, rows, :]
                )
        for half in range(2):
            state_out[filt, side * TILES + tile, half * 8 : half * 8 + 8, :] = running[half]

    def local_output(filt, side, tile, xs, ys):
        for pole in range(POLES):
            a = row8(rate, filt, side, tile, pole)
            w = row8(weight, filt, side, tile, pole)
            state = inits[side, tile, pole * SUBS : (pole + 1) * SUBS, :]
            for step in step_order(side):
                state = a * state + xs[step]
                term = w * state
                ys[step] = term if ys[step] is None else ys[step] + term
        return ys

    def correct(filt, side, tile, ys):
        decay = params[filt, side, 0, tile]
        a_sub = jnp.exp(-float(STEPS) * decay)
        term = weight[filt, side, tile] * carry_in[filt, side * TILES + tile]
        for sub in sub_order(side):
            for half in range(2):
                corr[side, pl.ds(half * 64 + sub, 8, stride=SUBS), :] = term[
                    half * 8 : half * 8 + 8
                ]
            term = a_sub * term
        for pole in range(POLES):
            a = row8(rate, filt, side, tile, pole)
            part = corr[side, pole * SUBS : (pole + 1) * SUBS, :]
            for step in step_order(side):
                part = a * part
                ys[step] = ys[step] + part
        return ys

    def send_state(filt, index):
        @pl.when(index != slot)
        def _():
            pltpu.make_async_remote_copy(
                src_ref=state_out.at[filt, index],
                dst_ref=state_in.at[filt, slot],
                send_sem=st_send.at[filt],
                recv_sem=st_recv.at[filt],
                device_id={"ctx": plane * GROUP + index},
                device_id_type=MESH,
            ).start()

        @pl.when(index == slot)
        def _():
            state_in[filt, slot] = state_out[filt, slot]

    def wait_bytes(ref, sem):
        pltpu.make_async_copy(ref, ref, sem).wait()

    def in_order(position, count):
        return position + my_dir * (count - 1 - 2 * position)

    def group_totals(filt):
        wait_bytes(state_in.at[filt, pl.ds(0, GROUP - 1)], st_recv.at[filt])
        a_chunk = jnp.exp(-float(CHUNK) * params[filt, my_dir, 0, my_tile])
        total = state_in[filt, in_order(0, GROUP)]
        for position in range(1, GROUP):
            total = a_chunk * total + state_in[filt, in_order(position, GROUP)]
        total_out[filt] = total
        total_in[filt, plane] = total
        for offset in range(1, PLANES):
            pltpu.make_async_remote_copy(
                src_ref=total_out.at[filt],
                dst_ref=total_in.at[filt, plane],
                send_sem=tot_send.at[filt],
                recv_sem=tot_recv.at[filt],
                device_id={"ctx": lax.rem(plane + offset, PLANES) * GROUP + slot},
                device_id_type=MESH,
            ).start()

    def carries(filt):
        wait_bytes(total_in.at[filt, pl.ds(0, PLANES - 1)], tot_recv.at[filt])
        decay = params[filt, my_dir, 0, my_tile]
        a_chunk = jnp.exp(-float(CHUNK) * decay)
        a_group = jnp.exp(-float(CHUNK * GROUP) * decay)
        mine = in_order(plane, PLANES)
        carry = jnp.zeros((POLES, LANES), F32)
        for position in range(PLANES - 1):
            further = a_group * carry + total_in[filt, in_order(position, PLANES)]
            carry = jnp.where(position < mine, further, carry)
        for position in range(GROUP):
            index = in_order(position, GROUP)
            carry_out[filt, index] = carry
            carry = a_chunk * carry + state_in[filt, index]
        for offset in range(1, GROUP):
            index = lax.rem(slot + offset, GROUP)
            pltpu.make_async_remote_copy(
                src_ref=carry_out.at[filt, index],
                dst_ref=carry_in.at[filt, slot],
                send_sem=car_send.at[filt],
                recv_sem=car_recv.at[filt],
                device_id={"ctx": plane * GROUP + index},
                device_id_type=MESH,
            ).start()
        carry_in[filt, slot] = carry_out[filt, slot]

    def wait_carries(filt):
        wait_bytes(carry_in.at[filt, pl.ds(0, GROUP - 1)], car_recv.at[filt])

    def loop_tiles(body):
        def step(tile, done):
            body(tile)
            return done

        lax.fori_loop(0, TILES, step, 0)

    derive(0, 0)
    loads[2].wait()
    for tile in range(TILES):
        v4[tile] = vals_s[:, tile * LANES : (tile + 1) * LANES].astype(F32)

    def first_states(side):
        def body(tile):
            chunk_states(0, side, tile, [picked(v4, tile, step) for step in range(STEPS)])
            send_state(0, side * TILES + tile)

        return body

    loop_tiles(first_states(0))
    par_copies[0].wait_recv()
    derive(0, 1)
    loop_tiles(first_states(1))

    w_core.wait_recv()
    w_chip[0:4, :] = w_pair[0]
    w_chip[4:8, :] = w_pair[1]
    for part in range(2):
        columns = pl.ds(pl.multiple_of((2 * core + part) * WIDTH, WIDTH), WIDTH)
        w_planes[z_hi, part] = w_chip[:, columns].astype(BF16)
    for offset in range(1, 4):
        pltpu.make_async_remote_copy(
            src_ref=w_planes.at[z_hi],
            dst_ref=w_planes.at[z_hi],
            send_sem=w_send.at[1],
            recv_sem=w_recv.at[1],
            device_id={"ctx": plane * GROUP + lax.rem(z_hi + offset, 4) * 2 + core},
            device_id_type=MESH,
        ).start()

    def first_output(side):
        def body(tile):
            xs = [picked(v4, tile, step) for step in range(STEPS)]
            ys = local_output(0, side, tile, xs, [None] * STEPS)
            for step in range(STEPS):
                y4[side, tile, step] = ys[step]

        return body

    loop_tiles(first_output(0))
    group_totals(0)
    derive(1, 0)
    loads[4].wait()
    loads[5].wait()
    for tile in range(TILES):
        g4[tile] = gate_s[:, tile * LANES : (tile + 1) * LANES].astype(F32)
        p4[tile] = post_s[:, tile * LANES : (tile + 1) * LANES].astype(F32)
    loop_tiles(first_output(1))
    par_copies[1].wait_recv()
    derive(1, 1)
    carries(0)

    wait_bytes(w_planes.at[pl.ds(0, 3)], w_recv.at[1])
    for part in range(2):
        for other in range(4):
            w_rows[other * 8 : other * 8 + 8, :] = w_planes[other, part].astype(F32)
        w_full[2 * core + part, plane] = w_rows[...].astype(BF16)
    for offset in range(1, PLANES):
        pltpu.make_async_remote_copy(
            src_ref=w_full.at[pl.ds(2 * core, 2), plane],
            dst_ref=w_full.at[pl.ds(2 * core, 2), plane],
            send_sem=w_send.at[2],
            recv_sem=w_recv.at[2],
            device_id={"ctx": lax.rem(plane + offset, PLANES) * GROUP + slot},
            device_id_type=MESH,
        ).start()

    wait_carries(0)

    def second_states(tile):
        for side in range(2):
            ys = [y4[side, tile, step] for step in range(STEPS)]
            ys = correct(0, side, tile, ys)
            for step in range(STEPS):
                ys[step] = ys[step] * picked(g4, tile, step)
                u4[side, tile, step] = ys[step]
            chunk_states(1, side, tile, ys)
            send_state(1, side * TILES + tile)

    loop_tiles(second_states)

    def second_output(side):
        def body(tile):
            xs = [u4[side, tile, step] for step in range(STEPS)]
            ys = [None] * STEPS if side == 0 else [y4[0, tile, step] for step in range(STEPS)]
            ys = local_output(1, side, tile, xs, ys)
            for step in range(STEPS):
                y4[0, tile, step] = ys[step]

        return body

    loop_tiles(second_output(0))
    group_totals(1)
    loop_tiles(second_output(1))
    carries(1)

    wait_bytes(w_full.at[pl.ds(0, 2), pl.ds(0, PLANES - 1)], w_recv.at[2])
    w_half = pltpu.make_async_remote_copy(
        src_ref=w_full.at[pl.ds(2 * core, 2)],
        dst_ref=w_full.at[pl.ds(2 * core, 2)],
        send_sem=w_send.at[3],
        recv_sem=w_recv.at[3],
        device_id={"ctx": ctx + 1 - 2 * core},
        device_id_type=MESH,
    )
    w_half.start()
    wait_carries(1)

    def finish(tile):
        ys = [y4[0, tile, step] for step in range(STEPS)]
        for side in range(2):
            ys = correct(1, side, tile, ys)
        for step in range(STEPS):
            mix_f32[pl.ds(step, SUBS, stride=STEPS), :] = ys[step] * picked(p4, tile, step)
        columns = pl.ds(pl.multiple_of(tile * LANES, LANES), LANES)
        mix[tp, :, columns] = mix_f32[...].astype(BF16)
        for offset in range(1, TP):
            pltpu.make_async_remote_copy(
                src_ref=mix.at[tp, :, columns],
                dst_ref=mix.at[tp, :, columns],
                send_sem=mix_send,
                recv_sem=mix_recv.at[tp],
                device_id={"tp": lax.rem(tp + offset, TP)},
                device_id_type=MESH,
            ).start()

    loop_tiles(finish)
    w_half.wait_recv()

    def product(block):
        return lax.dot_general(
            mix[block],
            w_full[block].reshape(WIDTH, WIDTH),
            (((1,), (1,)), ((), ())),
            preferred_element_type=F32,
        )

    acc[...] = product(tp)
    for offset in range(1, TP):
        block = lax.rem(tp + offset, TP)
        wait_bytes(mix.at[block], mix_recv.at[block])
        acc[...] += product(block)
    out_ref[...] = acc[...].astype(BF16)

    for copy in par_copies:
        copy.wait_send()
    w_core.wait_send()
    w_half.wait_send()
    wait_bytes(w_planes.at[pl.ds(0, 3)], w_send.at[1])
    wait_bytes(w_full.at[pl.ds(0, 2), pl.ds(0, PLANES - 1)], w_send.at[2])
    for filt in range(2):
        wait_bytes(state_in.at[filt, pl.ds(0, GROUP - 1)], st_send.at[filt])
        wait_bytes(total_in.at[filt, pl.ds(0, PLANES - 1)], tot_send.at[filt])
        wait_bytes(carry_in.at[filt, pl.ds(0, GROUP - 1)], car_send.at[filt])
    wait_bytes(mix.at[pl.ds(0, TP - 1)], mix_send)


def local(x_gate, x_post, values, decay, residue, w_out):
    block = (POLES, LANES)
    dma = pltpu.SemaphoreType.DMA
    scratch = [
        pltpu.VMEM((CHUNK, WIDTH), BF16),
        pltpu.VMEM((CHUNK, WIDTH), BF16),
        pltpu.VMEM((CHUNK, WIDTH), BF16),
        pltpu.VMEM((2, WIDTH, POLES), F32),
        pltpu.VMEM((2, WIDTH, POLES), F32),
        pltpu.VMEM((4, TP * WIDTH), BF16),
        pltpu.VMEM((2, 2, 2, TILES) + block, F32),
        pltpu.VMEM((2, 2, TILES) + block, F32),
        pltpu.VMEM((2, 2, TILES) + block, F32),
        pltpu.VMEM((2, 2, TILES) + block, F32),
        pltpu.VMEM((TILES, CHUNK, LANES), F32),
        pltpu.VMEM((TILES, CHUNK, LANES), F32),
        pltpu.VMEM((TILES, CHUNK, LANES), F32),
        pltpu.VMEM((2, TILES, STEPS, SUBS, LANES), F32),
        pltpu.VMEM((2, TILES, STEPS, SUBS, LANES), F32),
        pltpu.VMEM((2, POLES * SUBS, LANES), F32),
        pltpu.VMEM((2, TILES, POLES * SUBS, LANES), F32),
        pltpu.VMEM((2, POLES * SUBS, LANES), F32),
        pltpu.VMEM((2, GROUP) + block, F32),
        pltpu.VMEM((2, GROUP) + block, F32),
        pltpu.VMEM((2,) + block, F32),
        pltpu.VMEM((2, PLANES) + block, F32),
        pltpu.VMEM((2, GROUP) + block, F32),
        pltpu.VMEM((2, GROUP) + block, F32),
        pltpu.VMEM((2, 4, TP * WIDTH), F32),
        pltpu.VMEM((8, TP * WIDTH), F32),
        pltpu.VMEM((4, 2, 8, WIDTH), BF16),
        pltpu.VMEM((32, WIDTH), F32),
        pltpu.VMEM((TP, PLANES, 32, WIDTH), BF16),
        pltpu.VMEM((CHUNK, LANES), F32),
        pltpu.VMEM((TP, CHUNK, WIDTH), BF16),
        pltpu.VMEM((CHUNK, WIDTH), F32),
        dma((6,)),
        dma((2,)),
        dma((2,)),
        dma((2,)),
        dma((2,)),
        dma((2,)),
        dma((2,)),
        dma((2,)),
        dma((2,)),
        dma((4,)),
        dma((4,)),
        dma,
        dma((TP,)),
    ]
    return pl.pallas_call(
        mixer_kernel,
        out_shape=jax.ShapeDtypeStruct((CHUNK, WIDTH), BF16),
        in_specs=[pl.BlockSpec(memory_space=pl.ANY)] * 6,
        out_specs=pl.BlockSpec(memory_space=pltpu.VMEM),
        scratch_shapes=scratch,
        compiler_params=pltpu.CompilerParams(
            collective_id=0, has_side_effects=True, vmem_limit_bytes=48 * 1024 * 1024
        ),
        name="mixer",
    )(x_gate, x_post, values, decay, residue, w_out)


def solution(mesh):
    in_specs = (
        P("ctx", "tp"),
        P("ctx", "tp"),
        P("ctx", "tp"),
        P(None, "tp", None),
        P(None, "tp", None),
        P(("tp", "ctx"), None),
    )
    return jax.shard_map(
        local, mesh=mesh, in_specs=in_specs, out_specs=P("ctx", "tp"), check_vma=False
    )
```

time: 472 us -> 81.5 us (0.17)
  the two profiles are of different devices: /device:TPU:8 before, /device:TPU:1 now
where the time goes in v1:
time: 81.5 us; the launch traced here: 81.3 us
  Pallas kernels  78.5 us (96%)
  local copies, waits for them, and re-layouts  2.73 us (3%)
    pallas_call x1, Pallas kernels, local(): pl.pallas_call(mixer_kernel, out_shape=jax.ShapeDtypeStruct((CHUNK, WIDTH...  78.5 us
    unnamed x13, local copies, waits for them, and re-layouts  2.73 us

profile of v1, /device:TPU:1, one launch (start us, length us, event | category | flops | bytes accessed | tf_op | source)
XLA Modules:
  0.0 81.3 jit_solution(14698105445297427722)
XLA Ops:
  0.0 0.0 copy-start.4
  0.0 1.1 %copy.7.decay_hbm = f32[2,512,16]{2,1,0:T(8,128)S(1)} copy(f32[2,512,16]{1,2,0:T(8,128)} %param.9) | data formatting | bytes 131072 | tf_op args[3]
  1.1 0.0 copy-done.4
  1.1 0.0 copy-start
  1.1 0.0 copy-start.1
  1.1 0.0 copy-start.2
  1.1 0.0 copy-start.3
  1.1 0.2 copy.8.residue_hbm
  1.3 0.7 copy-done
  2.0 0.1 copy-done.1
  2.1 0.1 copy-done.2
  2.1 0.0 copy-done.3
  2.1 78.5 %mixer.1 = bf16[128,512]{1,0:T(8,128)(2,1)S(1)} custom-call(bf16[128,512]{1,0:T(8,128)(2,1)S(1)} %copy-done, bf16[128,512]{1,0:T(8,128)(2,1)S(1)} %copy-done.1, bf16[128,512]{1,0:T(8,128)(2,1)S(1)} %copy-done.2, f32[2,512,16]{2,1,0:T(8,128)S(1)} %copy.7.decay_hbm, f32[2,512,16]{2,1,0:T(8,128)S(1)} %copy.8.residue_hbm, bf16[4,2048]{1,0:T(4,128)(2,1)S(1)} %copy-done.3), custom_call_target="tpu_custom_call" | custom-call | tf_op jit(solution)/shard_map/mixer/pallas_call | solution.py:514
  80.7 0.7 copy.10
Async XLA Ops:
  0.0 1.1 %copy-start.4 = (f32[2,512,16]{1,2,0:T(8,128)S(1)}, f32[2,512,16]{1,2,0:T(8,128)}, u32[]{:S(2)}) copy-start(f32[2,512,16]{1,2,0:T(8,128)} %param.10) | copy-start | bytes 196612
  1.1 0.9 %copy-start = (bf16[128,512]{1,0:T(8,128)(2,1)S(1)}, bf16[128,512]{1,0:T(8,128)(2,1)}, u32[]{:S(2)}) copy-start(bf16[128,512]{1,0:T(8,128)(2,1)} %gate_hbm.1) | copy-start | bytes 393220
  1.1 1.0 %copy-start.1 = (bf16[128,512]{1,0:T(8,128)(2,1)S(1)}, bf16[128,512]{1,0:T(8,128)(2,1)}, u32[]{:S(2)}) copy-start(bf16[128,512]{1,0:T(8,128)(2,1)} %post_hbm.1) | copy-start | bytes 393220
  1.1 1.0 %copy-start.2 = (bf16[128,512]{1,0:T(8,128)(2,1)S(1)}, bf16[128,512]{1,0:T(8,128)(2,1)}, u32[]{:S(2)}) copy-start(bf16[128,512]{1,0:T(8,128)(2,1)} %vals_hbm.1) | copy-start | bytes 393220
  1.1 1.0 %copy-start.3 = (bf16[4,2048]{1,0:T(4,128)(2,1)S(1)}, bf16[4,2048]{1,0:T(4,128)(2,1)}, u32[]{:S(2)}) copy-start(bf16[4,2048]{1,0:T(4,128)(2,1)} %w_hbm.1) | copy-start | bytes 49156

commit v2 on v0

v2 whole, which is shorter than its diff:
```python
import jax
import jax.numpy as jnp
from jax import lax
from jax.experimental import pallas as pl
from jax.experimental.pallas import tpu as pltpu
from jax.sharding import PartitionSpec as P

MESH = pl.DeviceIdType.MESH
F32 = jnp.float32
BF16 = jnp.bfloat16
HIGHEST = lax.Precision.HIGHEST

POLES = 16
CHUNK = 128
CHUNKS = 128
CHIPS = 64
OWN = 8
LANES = 128
TILES = 4
PLANES = 16
TP = 4
WIDTH = TILES * LANES


def far_first():
    def hops(step):
        x, y, z = (min(part, 4 - part) for part in step)
        return x + y + 4 * z

    steps = [(x, y, z) for x in range(4) for y in range(4) for z in range(4)]
    return sorted(steps[1:], key=hops, reverse=True)


STEPS = far_first()


def split(value):
    high = value.astype(BF16)
    return high, (value - high.astype(F32)).astype(BF16)


def matmul(left, right):
    return jnp.dot(left, right, preferred_element_type=F32)


def product3(left, right_high, right_low):
    high, low = split(left)
    return matmul(high, right_high) + (matmul(high, right_low) + matmul(low, right_high))


def mixer_kernel(
    gate_hbm,
    post_hbm,
    vals_hbm,
    decay_hbm,
    residue_hbm,
    w_hbm,
    out_ref,
    gate_s,
    post_s,
    vals_s,
    decay_s,
    residue_s,
    w_s,
    par_own,
    par_out,
    par_in,
    v_out,
    g_out,
    v_in,
    g_in,
    v_rows,
    g_rows,
    post_t,
    table_high,
    table_low,
    back_high,
    back_low,
    rates,
    y_rows,
    o_rows,
    y_give,
    y_take,
    y_out,
    y_in,
    w_pair,
    w_chip,
    w_planes,
    w_block,
    w_full,
    mix_f32,
    mix,
    acc,
    load_sem,
    par_send,
    par_recv,
    v_send,
    v_recv,
    g_send,
    g_recv,
    near_send,
    near_recv,
    out_send,
    out_recv,
    w_send,
    w_recv,
    mix_send,
    mix_recv,
):
    ctx = lax.axis_index("ctx")
    tp = lax.axis_index("tp")
    core = lax.rem(ctx, 2)
    chip = ctx // 2
    z_hi = lax.rem(chip, 4)
    y_pos = lax.rem(chip // 4, 4)
    x_pos = chip // 16
    plane = chip // 4
    sibling = {"ctx": ctx + 1 - 2 * core}

    def moved(step):
        x = lax.rem(x_pos + step[0], 4)
        y = lax.rem(y_pos + step[1], 4)
        z = lax.rem(z_hi + step[2], 4)
        return x * 16 + y * 4 + z

    def same_core(other_chip):
        return {"ctx": other_chip * 2 + core}

    def remote(src, dst, send_sem, recv_sem, device):
        return pltpu.make_async_remote_copy(
            src_ref=src,
            dst_ref=dst,
            send_sem=send_sem,
            recv_sem=recv_sem,
            device_id=device,
            device_id_type=MESH,
        )

    def wait_bytes(ref, sem):
        pltpu.make_async_copy(ref, ref, sem).wait()

    loads = [
        pltpu.make_async_copy(src, dst, load_sem.at[index])
        for index, (src, dst) in enumerate(
            [
                (vals_hbm, vals_s),
                (gate_hbm, gate_s),
                (decay_hbm, decay_s),
                (residue_hbm, residue_s),
                (w_hbm, w_s),
                (post_hbm, post_s),
            ]
        )
    ]
    for load in loads:
        load.start()

    barrier = pltpu.get_barrier_semaphore()
    for step in STEPS:
        pl.semaphore_signal(
            barrier, inc=1, device_id=same_core(moved(step)), device_id_type=MESH
        )
    for offset in range(1, TP):
        pl.semaphore_signal(
            barrier, inc=1, device_id={"tp": lax.rem(tp + offset, TP)}, device_id_type=MESH
        )
    pl.semaphore_signal(barrier, inc=1, device_id=sibling, device_id_type=MESH)

    def spread(source, target):
        for tile in range(TILES):
            columns = source[:, tile * LANES : (tile + 1) * LANES].astype(F32).T
            for part in range(LANES // OWN):
                target[tile * 16 + part] = columns[part * OWN : (part + 1) * OWN].astype(BF16)

    loads[0].wait()
    spread(vals_s, v_out)
    loads[1].wait()
    spread(gate_s, g_out)

    row_id = lax.broadcasted_iota(jnp.int32, (WIDTH, LANES), 0)
    own_id = lax.broadcasted_iota(jnp.int32, (WIDTH, LANES), 1) // POLES + chip * OWN
    picks = jnp.concatenate(
        [(row_id == own_id).astype(F32), (row_id == WIDTH - 1 - own_id).astype(F32)], axis=1
    )
    pole_mask = (
        lax.broadcasted_iota(jnp.int32, (2, POLES, LANES), 1)
        == lax.rem(lax.broadcasted_iota(jnp.int32, (2, POLES, LANES), 2), POLES)
    ).astype(F32)
    loads[2].wait()
    loads[3].wait()
    par_out[...] = jnp.zeros((8, LANES), F32)
    par_own[...] = jnp.zeros((8, LANES), F32)
    for which, source in enumerate((decay_s, residue_s)):
        both = lax.dot_general(
            source[...].reshape(2 * POLES, WIDTH),
            picks,
            (((1,), (0,)), ((), ())),
            precision=HIGHEST,
            preferred_element_type=F32,
        )
        for target, part in ((par_own, both[:, :LANES]), (par_out, both[:, LANES:])):
            rows = jnp.sum(part.reshape(2, POLES, LANES) * pole_mask, axis=1)
            target[2 * which : 2 * which + 2, :] = rows
    loads[4].wait()
    w_pair[core] = w_s[...].astype(F32)

    pl.semaphore_wait(barrier, len(STEPS) + (TP - 1) + 1)

    par_copy = remote(par_out, par_in, par_send, par_recv, {"tp": TP - 1 - tp})
    par_copy.start()
    for step in STEPS:
        other = moved(step)
        remote(v_out.at[other], v_in.at[chip, core], v_send, v_recv, same_core(other)).start()
    w_core = remote(w_pair.at[core], w_pair.at[core], w_send.at[0], w_recv.at[0], sibling)
    w_core.start()
    for step in STEPS:
        other = moved(step)
        remote(g_out.at[other], g_in.at[chip, core], g_send, g_recv, same_core(other)).start()
    v_in[chip, core] = v_out[chip]
    g_in[chip, core] = g_out[chip]

    w_core.wait_recv()
    w_chip[0:4, :] = w_pair[0]
    w_chip[4:8, :] = w_pair[1]
    for part in range(2):
        columns = pl.ds(pl.multiple_of((2 * core + part) * WIDTH, WIDTH), WIDTH)
        w_planes[z_hi, part] = w_chip[:, columns].astype(BF16)
    for offset in range(1, 4):
        other = plane * 4 + lax.rem(z_hi + offset, 4)
        remote(
            w_planes.at[z_hi], w_planes.at[z_hi], w_send.at[1], w_recv.at[1], same_core(other)
        ).start()

    par_copy.wait_recv()
    poles = jnp.where(core == 1, par_in[...], par_own[...])
    square = (LANES, LANES)
    row = lax.broadcasted_iota(jnp.int32, square, 0)
    col = lax.broadcasted_iota(jnp.int32, square, 1)
    row_f = row.astype(F32)
    reverse = core == 1
    tap_power = jnp.where(reverse, jnp.where(row == 0, 0.0, CHUNK - row_f), row_f)
    out_power = jnp.where(reverse, CHUNK - row_f, row_f + 1.0)
    state_power = jnp.where(reverse, row_f, CHUNK - 1.0 - row_f)
    causal = (col - row) * (1 - 2 * core) >= 0
    channel_mask = (
        lax.broadcasted_iota(jnp.int32, (OWN, LANES), 1) // POLES
        == lax.broadcasted_iota(jnp.int32, (OWN, LANES), 0)
    ).astype(F32)

    def build(filt):
        decay = poles[filt : filt + 1, :]
        weight = poles[2 + filt : 3 + filt, :] * jnp.sqrt(2.0 * decay / POLES)
        rates[filt, 0:1, :] = decay
        taps = lax.dot_general(
            channel_mask,
            weight * jnp.exp(-decay * tap_power),
            (((1,), (1,)), ((), ())),
            precision=HIGHEST,
            preferred_element_type=F32,
        )
        to_states = jnp.exp(-decay * state_power)
        from_states = (weight * jnp.exp(-decay * out_power)).T
        for channel in range(OWN):
            line = jnp.broadcast_to(taps[channel : channel + 1, :], square)
            toeplitz = pltpu.roll(line, 0, 1, stride=1, stride_axis=0)
            high, low = split(jnp.where(causal, toeplitz, 0.0))
            table_high[filt, channel, :, :LANES] = high
            table_low[filt, channel, :, :LANES] = low
            high, low = split(jnp.where(col // POLES == channel, to_states, 0.0))
            table_high[filt, channel, :, LANES:] = high
            table_low[filt, channel, :, LANES:] = low
            high, low = split(jnp.where(row // POLES == channel, from_states, 0.0))
            back_high[filt, channel] = high
            back_low[filt, channel] = low

    build(0)
    build(1)
    loads[5].wait()
    for tile in range(TILES):
        post_t[tile] = post_s[:, tile * LANES : (tile + 1) * LANES].astype(F32).T

    def gather_rows(source, target):
        def body(other, done):
            for half in range(2):
                chunk = other * 2 + half
                place = chunk + core * (CHUNKS - 1 - 2 * chunk)
                rows = pl.ds(pl.multiple_of(place * OWN, OWN), OWN)
                target[rows, :] = source[other, half].astype(F32)
            return done

        lax.fori_loop(0, CHIPS, body, 0, unroll=8)

    def picked(ref, channel):
        return ref[pl.ds(channel, CHUNKS, stride=OWN), :]

    def near(ref, index):
        return remote(
            ref.at[:, core], ref.at[:, core], near_send.at[index], near_recv.at[index], sibling
        )

    def scan(states, filt):
        decay = rates[filt, 0:1, :]

        def later(value, count):
            return jnp.where(row >= count, pltpu.roll(value, count, 0), 0.0)

        value = later(states, 1)
        for power in range(7):
            count = 2**power
            value = value + jnp.exp(-float(CHUNK * count) * decay) * later(value, count)
        return value

    wait_bytes(v_in.at[pl.ds(0, CHIPS - 1), 0], v_recv)
    v_near = near(v_in, 0)
    v_near.start()
    v_near.wait_recv()
    gather_rows(v_in, v_rows)

    states = jnp.zeros(square, F32)
    for channel in range(OWN):
        line = picked(v_rows, channel).astype(BF16)
        both = matmul(line, table_high[0, channel]) + matmul(line, table_low[0, channel])
        y_rows[channel] = both[:, :LANES]
        states = states + both[:, LANES:]
    wait_bytes(g_in.at[pl.ds(0, CHIPS - 1), 0], g_recv)
    g_near = near(g_in, 1)
    g_near.start()
    carry = scan(states, 0)
    g_near.wait_recv()
    gather_rows(g_in, g_rows)

    states = jnp.zeros(square, F32)
    for channel in range(OWN):
        value = y_rows[channel] + product3(carry, back_high[0, channel], back_low[0, channel])
        value = value * picked(g_rows, channel)
        both = product3(value, table_high[1, channel], table_low[1, channel])
        y_rows[channel] = both[:, :LANES]
        states = states + both[:, LANES:]
    carry = scan(states, 1)
    for channel in range(OWN):
        value = y_rows[channel] + product3(carry, back_high[1, channel], back_low[1, channel])
        o_rows[pl.ds(channel, CHUNKS, stride=OWN), :] = value

    for part in range(CHIPS):
        y_give[part] = o_rows[(2 * part + 1) * OWN : (2 * part + 2) * OWN, :]
    y_near = remote(y_give, y_take, near_send.at[2], near_recv.at[2], sibling)
    y_near.start()

    wait_bytes(w_planes.at[pl.ds(0, 3)], w_recv.at[1])
    for part in range(2):
        for other in range(4):
            w_block[other * 8 : other * 8 + 8, :] = w_planes[other, part].astype(F32)
        w_full[2 * core + part, plane] = w_block[...].astype(BF16)

    y_near.wait_recv()
    for part in range(CHIPS):
        place = part + core * (CHIPS - 1 - 2 * part)
        total = o_rows[2 * part * OWN : (2 * part + 1) * OWN, :] + y_take[CHIPS - 1 - part]
        y_out[place] = total.astype(BF16)
    for step in STEPS:
        other = moved(step)
        remote(
            y_out.at[other], y_in.at[chip], out_send, out_recv.at[x_pos], same_core(other)
        ).start()
    y_in[chip] = y_out[chip]
    for offset in range(1, PLANES):
        other = lax.rem(plane + offset, PLANES) * 4 + z_hi
        remote(
            w_full.at[pl.ds(2 * core, 2), plane],
            w_full.at[pl.ds(2 * core, 2), plane],
            w_send.at[2],
            w_recv.at[2],
            same_core(other),
        ).start()

    for offset in range(TILES):
        tile = lax.rem(x_pos + offset, TILES)
        wait_bytes(y_in.at[pl.ds(0, 15 if offset == 0 else 16)], out_recv.at[tile])
        for part in range(16):
            mix_f32[part * OWN : (part + 1) * OWN, :] = (
                y_in[tile * 16 + part].astype(F32)
                * post_t[tile, part * OWN : (part + 1) * OWN, :]
            )
        rows = pl.ds(pl.multiple_of(tile * LANES, LANES), LANES)
        mix[tp, rows, :] = mix_f32[...].astype(BF16)
        for other in range(1, TP):
            remote(
                mix.at[tp, rows],
                mix.at[tp, rows],
                mix_send,
                mix_recv.at[tp],
                {"tp": lax.rem(tp + other, TP)},
            ).start()

    wait_bytes(w_full.at[pl.ds(0, 2), pl.ds(0, PLANES - 1)], w_recv.at[2])
    w_half = remote(
        w_full.at[pl.ds(2 * core, 2)],
        w_full.at[pl.ds(2 * core, 2)],
        w_send.at[3],
        w_recv.at[3],
        sibling,
    )
    w_half.start()
    w_half.wait_recv()

    def project(block):
        return matmul(w_full[block].reshape(WIDTH, WIDTH), mix[block])

    acc[...] = project(tp)
    for offset in range(1, TP):
        block = lax.rem(tp + offset, TP)
        wait_bytes(mix.at[block], mix_recv.at[block])
        acc[...] += project(block)
    for tile in range(TILES):
        rows = slice(tile * LANES, (tile + 1) * LANES)
        out_ref[:, rows] = acc[rows, :].T.astype(BF16)

    par_copy.wait_send()
    wait_bytes(v_in.at[pl.ds(0, CHIPS - 1), 0], v_send)
    wait_bytes(g_in.at[pl.ds(0, CHIPS - 1), 0], g_send)
    v_near.wait_send()
    g_near.wait_send()
    y_near.wait_send()
    wait_bytes(y_in.at[pl.ds(0, CHIPS - 1)], out_send)
    w_core.wait_send()
    wait_bytes(w_planes.at[pl.ds(0, 3)], w_send.at[1])
    wait_bytes(w_full.at[pl.ds(0, 2), pl.ds(0, PLANES - 1)], w_send.at[2])
    w_half.wait_send()
    wait_bytes(mix.at[pl.ds(0, TP - 1)], mix_send)


def local(x_gate, x_post, values, decay, residue, w_out):
    dma = pltpu.SemaphoreType.DMA
    scratch = [
        pltpu.VMEM((CHUNK, WIDTH), BF16),
        pltpu.VMEM((CHUNK, WIDTH), BF16),
        pltpu.VMEM((CHUNK, WIDTH), BF16),
        pltpu.VMEM((2, POLES, WIDTH), F32),
        pltpu.VMEM((2, POLES, WIDTH), F32),
        pltpu.VMEM((4, TP * WIDTH), BF16),
        pltpu.VMEM((8, LANES), F32),
        pltpu.VMEM((8, LANES), F32),
        pltpu.VMEM((8, LANES), F32),
        pltpu.VMEM((CHIPS, OWN, CHUNK), BF16),
        pltpu.VMEM((CHIPS, OWN, CHUNK), BF16),
        pltpu.VMEM((CHIPS, 2, OWN, CHUNK), BF16),
        pltpu.VMEM((CHIPS, 2, OWN, CHUNK), BF16),
        pltpu.VMEM((CHUNKS * OWN, CHUNK), F32),
        pltpu.VMEM((CHUNKS * OWN, CHUNK), F32),
        pltpu.VMEM((TILES, LANES, CHUNK), F32),
        pltpu.VMEM((2, OWN, CHUNK, 2 * LANES), BF16),
        pltpu.VMEM((2, OWN, CHUNK, 2 * LANES), BF16),
        pltpu.VMEM((2, OWN, LANES, CHUNK), BF16),
        pltpu.VMEM((2, OWN, LANES, CHUNK), BF16),
        pltpu.VMEM((2, 8, LANES), F32),
        pltpu.VMEM((OWN, CHUNKS, CHUNK), F32),
        pltpu.VMEM((CHUNKS * OWN, CHUNK), F32),
        pltpu.VMEM((CHIPS, OWN, CHUNK), F32),
        pltpu.VMEM((CHIPS, OWN, CHUNK), F32),
        pltpu.VMEM((CHIPS, OWN, CHUNK), BF16),
        pltpu.VMEM((CHIPS, OWN, CHUNK), BF16),
        pltpu.VMEM((2, 4, TP * WIDTH), F32),
        pltpu.VMEM((8, TP * WIDTH), F32),
        pltpu.VMEM((4, 2, 8, WIDTH), BF16),
        pltpu.VMEM((32, WIDTH), F32),
        pltpu.VMEM((TP, PLANES, 32, WIDTH), BF16),
        pltpu.VMEM((LANES, CHUNK), F32),
        pltpu.VMEM((TP, WIDTH, CHUNK), BF16),
        pltpu.VMEM((WIDTH, CHUNK), F32),
        dma((6,)),
        dma,
        dma,
        dma,
        dma,
        dma,
        dma,
        dma((3,)),
        dma((3,)),
        dma,
        dma((TILES,)),
        dma((4,)),
        dma((4,)),
        dma,
        dma((TP,)),
    ]
    return pl.pallas_call(
        mixer_kernel,
        out_shape=jax.ShapeDtypeStruct((CHUNK, WIDTH), BF16),
        in_specs=[pl.BlockSpec(memory_space=pl.ANY)] * 6,
        out_specs=pl.BlockSpec(memory_space=pltpu.VMEM),
        scratch_shapes=scratch,
        compiler_params=pltpu.CompilerParams(
            collective_id=0, has_side_effects=True, vmem_limit_bytes=64 * 1024 * 1024
        ),
        name="mixer",
    )(
        x_gate,
        x_post,
        values,
        jnp.swapaxes(decay, 1, 2),
        jnp.swapaxes(residue, 1, 2),
        w_out,
    )


def solution(mesh):
    in_specs = (
        P("ctx", "tp"),
        P("ctx", "tp"),
        P("ctx", "tp"),
        P(None, "tp", None),
        P(None, "tp", None),
        P(("tp", "ctx"), None),
    )
    return jax.shard_map(
        local, mesh=mesh, in_specs=in_specs, out_specs=P("ctx", "tp"), check_vma=False
    )
```

time: 472 us -> 65.9 us (0.14)
  the two profiles are of different devices: /device:TPU:8 before, /device:TPU:2 now
where the time goes in v2:
time: 65.9 us; the launch traced here: 65.7 us
  Pallas kernels  64.2 us (97%)
  local copies, waits for them, and re-layouts  1.57 us (2%)
    pallas_call x1, Pallas kernels, local(): pl.pallas_call(mixer_kernel, out_shape=jax.ShapeDtypeStruct((CHUNK, WIDTH...  64.2 us
    unnamed x1, local copies, waits for them, and re-layouts  1.57 us

profile of v2, /device:TPU:2, one launch (start us, length us, event | category | flops | bytes accessed | tf_op | source)
XLA Modules:
  0.0 65.7 jit_solution(18213944492626282253)
XLA Ops:
  0.0 64.2 %mixer.1 = bf16[128,512]{1,0:T(8,128)(2,1)} custom-call(bf16[128,512]{1,0:T(8,128)(2,1)} %gate_hbm.1, bf16[128,512]{1,0:T(8,128)(2,1)} %post_hbm.1, bf16[128,512]{1,0:T(8,128)(2,1)} %vals_hbm.1, f32[2,16,512]{2,1,0:T(8,128)} %bitcast.2, f32[2,16,512]{2,1,0:T(8,128)} %bitcast.3, bf16[4,2048]{1,0:T(4,128)(2,1)} %w_hbm.1), custom_call_target="tpu_custom_call" | custom-call | tf_op jit(solution)/shard_map/mixer/pallas_call | solution.py:486
  64.2 1.6 %copy.8 = bf16[128,512]{1,0:T(8,128)(2,1)} copy(bf16[128,512]{1,0:T(8,128)(2,1)} %mixer.1) | data formatting | bytes 262144

commit v3 on v2

--- a/solution.py
+++ b/solution.py
@@ -65,10 +65,8 @@
     par_own,
     par_out,
     par_in,
-    v_out,
-    g_out,
-    v_in,
-    g_in,
+    vg_out,
+    vg_in,
     v_rows,
     g_rows,
     post_t,
@@ -94,10 +92,8 @@
     load_sem,
     par_send,
     par_recv,
-    v_send,
-    v_recv,
-    g_send,
-    g_recv,
+    vg_send,
+    vg_recv,
     near_send,
     near_recv,
     out_send,
@@ -116,6 +112,7 @@
     x_pos = chip // 16
     plane = chip // 4
     sibling = {"ctx": ctx + 1 - 2 * core}
+    tp_peers = (tp + 1 - 2 * lax.rem(tp, 2), lax.rem(tp + 2, TP), TP - 1 - tp)
 
     def moved(step):
         x = lax.rem(x_pos + step[0], 4)
@@ -160,22 +157,17 @@
         pl.semaphore_signal(
             barrier, inc=1, device_id=same_core(moved(step)), device_id_type=MESH
         )
-    for offset in range(1, TP):
-        pl.semaphore_signal(
-            barrier, inc=1, device_id={"tp": lax.rem(tp + offset, TP)}, device_id_type=MESH
-        )
+    for other in tp_peers:
+        pl.semaphore_signal(barrier, inc=1, device_id={"tp": other}, device_id_type=MESH)
     pl.semaphore_signal(barrier, inc=1, device_id=sibling, device_id_type=MESH)
 
-    def spread(source, target):
+    for which, source in enumerate((vals_s, gate_s)):
+        loads[which].wait()
         for tile in range(TILES):
             columns = source[:, tile * LANES : (tile + 1) * LANES].astype(F32).T
             for part in range(LANES // OWN):
-                target[tile * 16 + part] = columns[part * OWN : (part + 1) * OWN].astype(BF16)
-
-    loads[0].wait()
-    spread(vals_s, v_out)
-    loads[1].wait()
-    spread(gate_s, g_out)
+                piece = columns[part * OWN : (part + 1) * OWN]
+                vg_out[tile * 16 + part, which] = piece.astype(BF16)
 
     row_id = lax.broadcasted_iota(jnp.int32, (WIDTH, LANES), 0)
     own_id = lax.broadcasted_iota(jnp.int32, (WIDTH, LANES), 1) // POLES + chip * OWN
@@ -208,16 +200,12 @@
 
     par_copy = remote(par_out, par_in, par_send, par_recv, {"tp": TP - 1 - tp})
     par_copy.start()
-    for step in STEPS:
-        other = moved(step)
-        remote(v_out.at[other], v_in.at[chip, core], v_send, v_recv, same_core(other)).start()
     w_core = remote(w_pair.at[core], w_pair.at[core], w_send.at[0], w_recv.at[0], sibling)
     w_core.start()
     for step in STEPS:
         other = moved(step)
-        remote(g_out.at[other], g_in.at[chip, core], g_send, g_recv, same_core(other)).start()
-    v_in[chip, core] = v_out[chip]
-    g_in[chip, core] = g_out[chip]
+        remote(vg_out.at[other], vg_in.at[chip, core], vg_send, vg_recv, same_core(other)).start()
+    vg_in[chip, core] = vg_out[chip]
 
     w_core.wait_recv()
     w_chip[0:4, :] = w_pair[0]
@@ -279,13 +267,13 @@
     for tile in range(TILES):
         post_t[tile] = post_s[:, tile * LANES : (tile + 1) * LANES].astype(F32).T
 
-    def gather_rows(source, target):
+    def gather_rows(which, target):
         def body(other, done):
             for half in range(2):
                 chunk = other * 2 + half
                 place = chunk + core * (CHUNKS - 1 - 2 * chunk)
                 rows = pl.ds(pl.multiple_of(place * OWN, OWN), OWN)
-                target[rows, :] = source[other, half].astype(F32)
+                target[rows, :] = vg_in[other, half, which].astype(F32)
             return done
 
         lax.fori_loop(0, CHIPS, body, 0, unroll=8)
@@ -293,10 +281,9 @@
     def picked(ref, channel):
         return ref[pl.ds(channel, CHUNKS, stride=OWN), :]
 
-    def near(ref, index):
-        return remote(
-            ref.at[:, core], ref.at[:, core], near_send.at[index], near_recv.at[index], sibling
-        )
+    def near(which):
+        part = vg_in.at[:, core, which]
+        return remote(part, part, near_send.at[which], near_recv.at[which], sibling)
 
     def scan(states, filt):
         decay = rates[filt, 0:1, :]
@@ -310,11 +297,29 @@
             value = value + jnp.exp(-float(CHUNK * count) * decay) * later(value, count)
         return value
 
-    wait_bytes(v_in.at[pl.ds(0, CHIPS - 1), 0], v_recv)
-    v_near = near(v_in, 0)
+    wait_bytes(vg_in.at[pl.ds(0, CHIPS - 1), 0], vg_recv)
+    v_near = near(0)
     v_near.start()
+    g_near = near(1)
+    g_near.start()
+
+    wait_bytes(w_planes.at[pl.ds(0, 3)], w_recv.at[1])
+    for part in range(2):
+        for other in range(4):
+            w_block[other * 8 : other * 8 + 8, :] = w_planes[other, part].astype(F32)
+        w_full[2 * core + part, plane] = w_block[...].astype(BF16)
+    for offset in range(1, PLANES):
+        other = lax.rem(plane + offset, PLANES) * 4 + z_hi
+        remote(
+            w_full.at[pl.ds(2 * core, 2), plane],
+            w_full.at[pl.ds(2 * core, 2), plane],
+            w_send.at[2],
+            w_recv.at[2],
+            same_core(other),
+        ).start()
+
     v_near.wait_recv()
-    gather_rows(v_in, v_rows)
+    gather_rows(0, v_rows)
 
     states = jnp.zeros(square, F32)
     for channel in range(OWN):
@@ -322,12 +327,9 @@
         both = matmul(line, table_high[0, channel]) + matmul(line, table_low[0, channel])
         y_rows[channel] = both[:, :LANES]
         states = states + both[:, LANES:]
-    wait_bytes(g_in.at[pl.ds(0, CHIPS - 1), 0], g_recv)
-    g_near = near(g_in, 1)
-    g_near.start()
     carry = scan(states, 0)
     g_near.wait_recv()
-    gather_rows(g_in, g_rows)
+    gather_rows(1, g_rows)
 
     states = jnp.zeros(square, F32)
     for channel in range(OWN):
@@ -346,12 +348,6 @@
     y_near = remote(y_give, y_take, near_send.at[2], near_recv.at[2], sibling)
     y_near.start()
 
-    wait_bytes(w_planes.at[pl.ds(0, 3)], w_recv.at[1])
-    for part in range(2):
-        for other in range(4):
-            w_block[other * 8 : other * 8 + 8, :] = w_planes[other, part].astype(F32)
-        w_full[2 * core + part, plane] = w_block[...].astype(BF16)
-
     y_near.wait_recv()
     for part in range(CHIPS):
         place = part + core * (CHIPS - 1 - 2 * part)
@@ -363,15 +359,16 @@
             y_out.at[other], y_in.at[chip], out_send, out_recv.at[x_pos], same_core(other)
         ).start()
     y_in[chip] = y_out[chip]
-    for offset in range(1, PLANES):
-        other = lax.rem(plane + offset, PLANES) * 4 + z_hi
-        remote(
-            w_full.at[pl.ds(2 * core, 2), plane],
-            w_full.at[pl.ds(2 * core, 2), plane],
-            w_send.at[2],
-            w_recv.at[2],
-            same_core(other),
-        ).start()
+
+    wait_bytes(w_full.at[pl.ds(0, 2), pl.ds(0, PLANES - 1)], w_recv.at[2])
+    w_half = remote(
+        w_full.at[pl.ds(2 * core, 2)],
+        w_full.at[pl.ds(2 * core, 2)],
+        w_send.at[3],
+        w_recv.at[3],
+        sibling,
+    )
+    w_half.start()
 
     for offset in range(TILES):
         tile = lax.rem(x_pos + offset, TILES)
@@ -383,32 +380,18 @@
             )
         rows = pl.ds(pl.multiple_of(tile * LANES, LANES), LANES)
         mix[tp, rows, :] = mix_f32[...].astype(BF16)
-        for other in range(1, TP):
+        for other in reversed(tp_peers):
             remote(
-                mix.at[tp, rows],
-                mix.at[tp, rows],
-                mix_send,
-                mix_recv.at[tp],
-                {"tp": lax.rem(tp + other, TP)},
+                mix.at[tp, rows], mix.at[tp, rows], mix_send, mix_recv.at[tp], {"tp": other}
             ).start()
 
-    wait_bytes(w_full.at[pl.ds(0, 2), pl.ds(0, PLANES - 1)], w_recv.at[2])
-    w_half = remote(
-        w_full.at[pl.ds(2 * core, 2)],
-        w_full.at[pl.ds(2 * core, 2)],
-        w_send.at[3],
-        w_recv.at[3],
-        sibling,
-    )
-    w_half.start()
     w_half.wait_recv()
 
     def project(block):
         return matmul(w_full[block].reshape(WIDTH, WIDTH), mix[block])
 
     acc[...] = project(tp)
-    for offset in range(1, TP):
-        block = lax.rem(tp + offset, TP)
+    for block in tp_peers:
         wait_bytes(mix.at[block], mix_recv.at[block])
         acc[...] += project(block)
     for tile in range(TILES):
@@ -416,8 +399,7 @@
         out_ref[:, rows] = acc[rows, :].T.astype(BF16)
 
     par_copy.wait_send()
-    wait_bytes(v_in.at[pl.ds(0, CHIPS - 1), 0], v_send)
-    wait_bytes(g_in.at[pl.ds(0, CHIPS - 1), 0], g_send)
+    wait_bytes(vg_in.at[pl.ds(0, CHIPS - 1), 0], vg_send)
     v_near.wait_send()
     g_near.wait_send()
     y_near.wait_send()
@@ -441,10 +423,8 @@
         pltpu.VMEM((8, LANES), F32),
         pltpu.VMEM((8, LANES), F32),
         pltpu.VMEM((8, LANES), F32),
-        pltpu.VMEM((CHIPS, OWN, CHUNK), BF16),
-        pltpu.VMEM((CHIPS, OWN, CHUNK), BF16),
         pltpu.VMEM((CHIPS, 2, OWN, CHUNK), BF16),
-        pltpu.VMEM((CHIPS, 2, OWN, CHUNK), BF16),
+        pltpu.VMEM((CHIPS, 2, 2, OWN, CHUNK), BF16),
         pltpu.VMEM((CHUNKS * OWN, CHUNK), F32),
         pltpu.VMEM((CHUNKS * OWN, CHUNK), F32),
         pltpu.VMEM((TILES, LANES, CHUNK), F32),
@@ -472,8 +452,6 @@
         dma,
         dma,
         dma,
-        dma,
-        dma,
         dma((3,)),
         dma((3,)),
         dma,
@@ -490,16 +468,21 @@
         out_specs=pl.BlockSpec(memory_space=pltpu.VMEM),
         scratch_shapes=scratch,
         compiler_params=pltpu.CompilerParams(
-            collective_id=0, has_side_effects=True, vmem_limit_bytes=64 * 1024 * 1024
+            collective_id=0, has_side_effects=True, vmem_limit_bytes=48 * 1024 * 1024
         ),
         name="mixer",
     )(
-        x_gate,
-        x_post,
-        values,
-        jnp.swapaxes(decay, 1, 2),
-        jnp.swapaxes(residue, 1, 2),
-        w_out,
+        *(
+            pltpu.with_memory_space_constraint(array, pltpu.HBM)
+            for array in (
+                x_gate,
+                x_post,
+                values,
+                jnp.swapaxes(decay, 1, 2),
+                jnp.swapaxes(residue, 1, 2),
+                w_out,
+            )
+        )
     )
 
 

time: 65.9 us -> 66 us (level)
  the two profiles are of different devices: /device:TPU:2 before, /device:TPU:1 now
where the time goes in v3:
time: 66 us; the launch traced here: 65.9 us
  Pallas kernels  65.2 us (99%)
  local copies, waits for them, and re-layouts  0.66 us (1%)
    pallas_call x1, Pallas kernels, local(): pl.pallas_call(mixer_kernel, out_shape=jax.ShapeDtypeStruct((CHUNK, WIDTH...  65.2 us

profile of v3, /device:TPU:1, one launch (start us, length us, event | category | flops | bytes accessed | tf_op | source)
XLA Modules:
  0.0 65.9 jit_solution(16588726681829816344)
XLA Ops:
  0.0 65.2 %mixer.1 = bf16[128,512]{1,0:T(8,128)(2,1)S(1)} custom-call(bf16[128,512]{1,0:T(8,128)(2,1)} %gate_hbm.1, bf16[128,512]{1,0:T(8,128)(2,1)} %post_hbm.1, bf16[128,512]{1,0:T(8,128)(2,1)} %vals_hbm.1, f32[2,16,512]{2,1,0:T(8,128)} %bitcast.2, f32[2,16,512]{2,1,0:T(8,128)} %bitcast.3, bf16[4,2048]{1,0:T(4,128)(2,1)} %w_hbm.1), custom_call_target="tpu_custom_call" | custom-call | tf_op jit(solution)/shard_map/mixer/pallas_call | solution.py:464
  65.3 0.7 copy.8

commit v4 on v2

--- a/solution.py
+++ b/solution.py
@@ -32,6 +32,7 @@
 
 
 STEPS = far_first()
+PLANE_OFFSETS = [step[:2] for step in STEPS if step[2] == 0]
 
 
 def split(value):
@@ -83,14 +84,13 @@
     y_take,
     y_out,
     y_in,
-    w_pair,
-    w_chip,
     w_planes,
     w_block,
     w_full,
     mix_f32,
     mix,
     acc,
+    sums,
     load_sem,
     par_send,
     par_recv,
@@ -116,6 +116,7 @@
     x_pos = chip // 16
     plane = chip // 4
     sibling = {"ctx": ctx + 1 - 2 * core}
+    tp_peers = (tp + 1 - 2 * lax.rem(tp, 2), lax.rem(tp + 2, TP), TP - 1 - tp)
 
     def moved(step):
         x = lax.rem(x_pos + step[0], 4)
@@ -160,10 +161,8 @@
         pl.semaphore_signal(
             barrier, inc=1, device_id=same_core(moved(step)), device_id_type=MESH
         )
-    for offset in range(1, TP):
-        pl.semaphore_signal(
-            barrier, inc=1, device_id={"tp": lax.rem(tp + offset, TP)}, device_id_type=MESH
-        )
+    for other in tp_peers:
+        pl.semaphore_signal(barrier, inc=1, device_id={"tp": other}, device_id_type=MESH)
     pl.semaphore_signal(barrier, inc=1, device_id=sibling, device_id_type=MESH)
 
     def spread(source, target):
@@ -202,7 +201,7 @@
             rows = jnp.sum(part.reshape(2, POLES, LANES) * pole_mask, axis=1)
             target[2 * which : 2 * which + 2, :] = rows
     loads[4].wait()
-    w_pair[core] = w_s[...].astype(F32)
+    w_planes[z_hi] = w_s[...]
 
     pl.semaphore_wait(barrier, len(STEPS) + (TP - 1) + 1)
 
@@ -211,25 +210,17 @@
     for step in STEPS:
         other = moved(step)
         remote(v_out.at[other], v_in.at[chip, core], v_send, v_recv, same_core(other)).start()
-    w_core = remote(w_pair.at[core], w_pair.at[core], w_send.at[0], w_recv.at[0], sibling)
-    w_core.start()
+    v_in[chip, core] = v_out[chip]
+
+    for offset in (2, 1, 3):
+        other = plane * 4 + lax.rem(z_hi + offset, 4)
+        remote(
+            w_planes.at[z_hi], w_planes.at[z_hi], w_send.at[0], w_recv.at[0], same_core(other)
+        ).start()
     for step in STEPS:
         other = moved(step)
         remote(g_out.at[other], g_in.at[chip, core], g_send, g_recv, same_core(other)).start()
-    v_in[chip, core] = v_out[chip]
     g_in[chip, core] = g_out[chip]
-
-    w_core.wait_recv()
-    w_chip[0:4, :] = w_pair[0]
-    w_chip[4:8, :] = w_pair[1]
-    for part in range(2):
-        columns = pl.ds(pl.multiple_of((2 * core + part) * WIDTH, WIDTH), WIDTH)
-        w_planes[z_hi, part] = w_chip[:, columns].astype(BF16)
-    for offset in range(1, 4):
-        other = plane * 4 + lax.rem(z_hi + offset, 4)
-        remote(
-            w_planes.at[z_hi], w_planes.at[z_hi], w_send.at[1], w_recv.at[1], same_core(other)
-        ).start()
 
     par_copy.wait_recv()
     poles = jnp.where(core == 1, par_in[...], par_own[...])
@@ -294,9 +285,8 @@
         return ref[pl.ds(channel, CHUNKS, stride=OWN), :]
 
     def near(ref, index):
-        return remote(
-            ref.at[:, core], ref.at[:, core], near_send.at[index], near_recv.at[index], sibling
-        )
+        part = ref.at[:, core]
+        return remote(part, part, near_send.at[index], near_recv.at[index], sibling)
 
     def scan(states, filt):
         decay = rates[filt, 0:1, :]
@@ -309,6 +299,20 @@
             count = 2**power
             value = value + jnp.exp(-float(CHUNK * count) * decay) * later(value, count)
         return value
+
+    wait_bytes(w_planes.at[pl.ds(0, 3)], w_recv.at[0])
+    for other in range(4):
+        w_block[other * 4 : other * 4 + 4, :] = w_planes[other].astype(F32)
+    for block in range(TP):
+        columns = slice(block * WIDTH, (block + 1) * WIDTH)
+        w_full[block, core, plane] = w_block[:, columns].astype(BF16)
+    for offset in PLANE_OFFSETS:
+        x = lax.rem(x_pos + offset[0], 4)
+        y = lax.rem(y_pos + offset[1], 4)
+        part = w_full.at[:, core, plane]
+        remote(
+            part, part, w_send.at[1], w_recv.at[1], same_core(x * 16 + y * 4 + z_hi)
+        ).start()
 
     wait_bytes(v_in.at[pl.ds(0, CHIPS - 1), 0], v_recv)
     v_near = near(v_in, 0)
@@ -322,10 +326,10 @@
         both = matmul(line, table_high[0, channel]) + matmul(line, table_low[0, channel])
         y_rows[channel] = both[:, :LANES]
         states = states + both[:, LANES:]
+    carry = scan(states, 0)
     wait_bytes(g_in.at[pl.ds(0, CHIPS - 1), 0], g_recv)
     g_near = near(g_in, 1)
     g_near.start()
-    carry = scan(states, 0)
     g_near.wait_recv()
     gather_rows(g_in, g_rows)
 
@@ -337,41 +341,47 @@
         y_rows[channel] = both[:, :LANES]
         states = states + both[:, LANES:]
     carry = scan(states, 1)
-    for channel in range(OWN):
-        value = y_rows[channel] + product3(carry, back_high[1, channel], back_low[1, channel])
-        o_rows[pl.ds(channel, CHUNKS, stride=OWN), :] = value
-
-    for part in range(CHIPS):
-        y_give[part] = o_rows[(2 * part + 1) * OWN : (2 * part + 2) * OWN, :]
-    y_near = remote(y_give, y_take, near_send.at[2], near_recv.at[2], sibling)
-    y_near.start()
-
-    wait_bytes(w_planes.at[pl.ds(0, 3)], w_recv.at[1])
-    for part in range(2):
-        for other in range(4):
-            w_block[other * 8 : other * 8 + 8, :] = w_planes[other, part].astype(F32)
-        w_full[2 * core + part, plane] = w_block[...].astype(BF16)
-
-    y_near.wait_recv()
-    for part in range(CHIPS):
-        place = part + core * (CHIPS - 1 - 2 * part)
-        total = o_rows[2 * part * OWN : (2 * part + 1) * OWN, :] + y_take[CHIPS - 1 - part]
-        y_out[place] = total.astype(BF16)
+
+    y_near = []
+    for half in range(2):
+        chunks = slice(half * CHIPS, (half + 1) * CHIPS)
+        parts = range(half * CHIPS // 2, (half + 1) * CHIPS // 2)
+        high, low = split(carry[chunks])
+        for channel in range(OWN):
+            value = y_rows[channel, chunks, :] + (
+                matmul(high, back_high[1, channel])
+                + (matmul(high, back_low[1, channel]) + matmul(low, back_high[1, channel]))
+            )
+            o_rows[pl.ds(half * CHIPS * OWN + channel, CHIPS, stride=OWN), :] = value
+        for part in parts:
+            y_give[part] = o_rows[(2 * part + 1) * OWN : (2 * part + 2) * OWN, :]
+        piece = pl.ds(half * CHIPS // 2, CHIPS // 2)
+        copy = remote(
+            y_give.at[piece],
+            y_take.at[piece],
+            near_send.at[2 + half],
+            near_recv.at[2 + half],
+            sibling,
+        )
+        copy.start()
+        y_near.append(copy)
+    for half in (1, 0):
+        y_near[1 - half].wait_recv()
+        for part in range(half * CHIPS // 2, (half + 1) * CHIPS // 2):
+            place = part + core * (CHIPS - 1 - 2 * part)
+            total = o_rows[2 * part * OWN : (2 * part + 1) * OWN, :] + y_take[CHIPS - 1 - part]
+            y_out[place] = total.astype(BF16)
     for step in STEPS:
         other = moved(step)
         remote(
             y_out.at[other], y_in.at[chip], out_send, out_recv.at[x_pos], same_core(other)
         ).start()
     y_in[chip] = y_out[chip]
-    for offset in range(1, PLANES):
-        other = lax.rem(plane + offset, PLANES) * 4 + z_hi
-        remote(
-            w_full.at[pl.ds(2 * core, 2), plane],
-            w_full.at[pl.ds(2 * core, 2), plane],
-            w_send.at[2],
-            w_recv.at[2],
-            same_core(other),
-        ).start()
+
+    wait_bytes(w_full.at[:, 0, pl.ds(0, PLANES - 1)], w_recv.at[1])
+    part = w_full.at[:, core]
+    w_half = remote(part, part, w_send.at[2], w_recv.at[2], sibling)
+    w_half.start()
 
     for offset in range(TILES):
         tile = lax.rem(x_pos + offset, TILES)
@@ -383,48 +393,38 @@
             )
         rows = pl.ds(pl.multiple_of(tile * LANES, LANES), LANES)
         mix[tp, rows, :] = mix_f32[...].astype(BF16)
-        for other in range(1, TP):
+        for other in reversed(tp_peers):
             remote(
-                mix.at[tp, rows],
-                mix.at[tp, rows],
-                mix_send,
-                mix_recv.at[tp],
-                {"tp": lax.rem(tp + other, TP)},
+                mix.at[tp, rows], mix.at[tp, rows], mix_send, mix_recv.at[tp], {"tp": other}
             ).start()
 
-    wait_bytes(w_full.at[pl.ds(0, 2), pl.ds(0, PLANES - 1)], w_recv.at[2])
-    w_half = remote(
-        w_full.at[pl.ds(2 * core, 2)],
-        w_full.at[pl.ds(2 * core, 2)],
-        w_send.at[3],
-        w_recv.at[3],
-        sibling,
-    )
-    w_half.start()
     w_half.wait_recv()
 
     def project(block):
         return matmul(w_full[block].reshape(WIDTH, WIDTH), mix[block])
 
     acc[...] = project(tp)
-    for offset in range(1, TP):
-        block = lax.rem(tp + offset, TP)
+    for block in tp_peers:
         wait_bytes(mix.at[block], mix_recv.at[block])
         acc[...] += project(block)
+    for group in range(CHIPS):
+        for part in range(2):
+            first = part * (WIDTH // 2) + group * 4
+            sums[group * 8 + part * 4 : group * 8 + part * 4 + 4, :] = acc[first : first + 4, :]
     for tile in range(TILES):
         rows = slice(tile * LANES, (tile + 1) * LANES)
-        out_ref[:, rows] = acc[rows, :].T.astype(BF16)
+        out_ref[:, rows] = sums[rows, :].T.astype(BF16)
 
     par_copy.wait_send()
     wait_bytes(v_in.at[pl.ds(0, CHIPS - 1), 0], v_send)
     wait_bytes(g_in.at[pl.ds(0, CHIPS - 1), 0], g_send)
     v_near.wait_send()
     g_near.wait_send()
-    y_near.wait_send()
+    for copy in y_near:
+        copy.wait_send()
     wait_bytes(y_in.at[pl.ds(0, CHIPS - 1)], out_send)
-    w_core.wait_send()
-    wait_bytes(w_planes.at[pl.ds(0, 3)], w_send.at[1])
-    wait_bytes(w_full.at[pl.ds(0, 2), pl.ds(0, PLANES - 1)], w_send.at[2])
+    wait_bytes(w_planes.at[pl.ds(0, 3)], w_send.at[0])
+    wait_bytes(w_full.at[:, 0, pl.ds(0, PLANES - 1)], w_send.at[1])
     w_half.wait_send()
     wait_bytes(mix.at[pl.ds(0, TP - 1)], mix_send)
 
@@ -459,14 +459,13 @@
         pltpu.VMEM((CHIPS, OWN, CHUNK), F32),
         pltpu.VMEM((CHIPS, OWN, CHUNK), BF16),
         pltpu.VMEM((CHIPS, OWN, CHUNK), BF16),
-        pltpu.VMEM((2, 4, TP * WIDTH), F32),
-        pltpu.VMEM((8, TP * WIDTH), F32),
-        pltpu.VMEM((4, 2, 8, WIDTH), BF16),
-        pltpu.VMEM((32, WIDTH), F32),
-        pltpu.VMEM((TP, PLANES, 32, WIDTH), BF16),
+        pltpu.VMEM((4, 4, TP * WIDTH), BF16),
+        pltpu.VMEM((16, TP * WIDTH), F32),
+        pltpu.VMEM((TP, 2, PLANES, 16, WIDTH), BF16),
         pltpu.VMEM((LANES, CHUNK), F32),
         pltpu.VMEM((TP, WIDTH, CHUNK), BF16),
         pltpu.VMEM((WIDTH, CHUNK), F32),
+        pltpu.VMEM((WIDTH, CHUNK), F32),
         dma((6,)),
         dma,
         dma,
@@ -474,12 +473,12 @@
         dma,
         dma,
         dma,
+        dma((4,)),
+        dma((4,)),
+        dma,
+        dma((TILES,)),
         dma((3,)),
         dma((3,)),
-        dma,
-        dma((TILES,)),
-        dma((4,)),
-        dma((4,)),
         dma,
         dma((TP,)),
     ]
@@ -490,16 +489,21 @@
         out_specs=pl.BlockSpec(memory_space=pltpu.VMEM),
         scratch_shapes=scratch,
         compiler_params=pltpu.CompilerParams(
-            collective_id=0, has_side_effects=True, vmem_limit_bytes=64 * 1024 * 1024
+            collective_id=0, has_side_effects=True, vmem_limit_bytes=48 * 1024 * 1024
         ),
         name="mixer",
     )(
-        x_gate,
-        x_post,
-        values,
-        jnp.swapaxes(decay, 1, 2),
-        jnp.swapaxes(residue, 1, 2),
-        w_out,
+        *(
+            pltpu.with_memory_space_constraint(array, pltpu.HBM)
+            for array in (
+                x_gate,
+                x_post,
+                values,
+                jnp.swapaxes(decay, 1, 2),
+                jnp.swapaxes(residue, 1, 2),
+                w_out,
+            )
+        )
     )
 
 

time: 65.9 us -> 65.9 us (level)
  the two profiles are of different devices: /device:TPU:2 before, /device:TPU:1 now
where the time goes in v4:
time: 65.9 us; the launch traced here: 65.7 us
  Pallas kernels  65.1 us (99%)
  local copies, waits for them, and re-layouts  0.66 us (1%)
    pallas_call x1, Pallas kernels, local(): pl.pallas_call(mixer_kernel, out_shape=jax.ShapeDtypeStruct((CHUNK, WIDTH...  65.1 us

profile of v4, /device:TPU:1, one launch (start us, length us, event | category | flops | bytes accessed | tf_op | source)
XLA Modules:
  0.0 65.7 jit_solution(11525177752518232841)
XLA Ops:
  0.0 65.1 %mixer.1 = bf16[128,512]{1,0:T(8,128)(2,1)S(1)} custom-call(bf16[128,512]{1,0:T(8,128)(2,1)} %gate_hbm.1, bf16[128,512]{1,0:T(8,128)(2,1)} %post_hbm.1, bf16[128,512]{1,0:T(8,128)(2,1)} %vals_hbm.1, f32[2,16,512]{2,1,0:T(8,128)} %bitcast.2, f32[2,16,512]{2,1,0:T(8,128)} %bitcast.3, bf16[4,2048]{1,0:T(4,128)(2,1)} %w_hbm.1), custom_call_target="tpu_custom_call" | custom-call | tf_op jit(solution)/shard_map/mixer/pallas_call | solution.py:485
  65.1 0.7 %copy.8 = bf16[128,512]{1,0:T(8,128)(2,1)} copy(bf16[128,512]{1,0:T(8,128)(2,1)S(1)} %mixer.1) | data formatting | bytes 262144

commit v5 on v4

--- a/solution.py
+++ b/solution.py
@@ -17,7 +17,6 @@
 OWN = 8
 LANES = 128
 TILES = 4
-PLANES = 16
 TP = 4
 WIDTH = TILES * LANES
 
@@ -32,7 +31,6 @@
 
 
 STEPS = far_first()
-PLANE_OFFSETS = [step[:2] for step in STEPS if step[2] == 0]
 
 
 def split(value):
@@ -305,14 +303,19 @@
         w_block[other * 4 : other * 4 + 4, :] = w_planes[other].astype(F32)
     for block in range(TP):
         columns = slice(block * WIDTH, (block + 1) * WIDTH)
-        w_full[block, core, plane] = w_block[:, columns].astype(BF16)
-    for offset in PLANE_OFFSETS:
-        x = lax.rem(x_pos + offset[0], 4)
-        y = lax.rem(y_pos + offset[1], 4)
-        part = w_full.at[:, core, plane]
-        remote(
-            part, part, w_send.at[1], w_recv.at[1], same_core(x * 16 + y * 4 + z_hi)
-        ).start()
+        w_full[block, core, x_pos, y_pos] = w_block[:, columns].astype(BF16)
+    blocks = (pl.ds(0, 2), pl.ds(2, 2))
+
+    def along(axis, part, sem):
+        for offset in (2, 1, 3):
+            x = lax.rem(x_pos + offset, 4) if axis == 0 else x_pos
+            y = lax.rem(y_pos + offset, 4) if axis == 1 else y_pos
+            remote(
+                part, part, w_send.at[sem], w_recv.at[sem], same_core(x * 16 + y * 4 + z_hi)
+            ).start()
+
+    along(1, w_full.at[blocks[0], core, x_pos, y_pos], 1)
+    along(0, w_full.at[blocks[1], core, x_pos, y_pos], 2)
 
     wait_bytes(v_in.at[pl.ds(0, CHIPS - 1), 0], v_recv)
     v_near = near(v_in, 0)
@@ -327,6 +330,10 @@
         y_rows[channel] = both[:, :LANES]
         states = states + both[:, LANES:]
     carry = scan(states, 0)
+    for half in range(2):
+        wait_bytes(w_full.at[blocks[half], 0, 0, pl.ds(0, 3)], w_recv.at[1 + half])
+    along(0, w_full.at[blocks[0], core, x_pos], 3)
+    along(1, w_full.at[blocks[1], core, :, y_pos], 4)
     wait_bytes(g_in.at[pl.ds(0, CHIPS - 1), 0], g_recv)
     g_near = near(g_in, 1)
     g_near.start()
@@ -378,9 +385,10 @@
         ).start()
     y_in[chip] = y_out[chip]
 
-    wait_bytes(w_full.at[:, 0, pl.ds(0, PLANES - 1)], w_recv.at[1])
+    for half in range(2):
+        wait_bytes(w_full.at[blocks[half], 0, pl.ds(0, 3)], w_recv.at[3 + half])
     part = w_full.at[:, core]
-    w_half = remote(part, part, w_send.at[2], w_recv.at[2], sibling)
+    w_half = remote(part, part, w_send.at[5], w_recv.at[5], sibling)
     w_half.start()
 
     for offset in range(TILES):
@@ -424,7 +432,9 @@
         copy.wait_send()
     wait_bytes(y_in.at[pl.ds(0, CHIPS - 1)], out_send)
     wait_bytes(w_planes.at[pl.ds(0, 3)], w_send.at[0])
-    wait_bytes(w_full.at[:, 0, pl.ds(0, PLANES - 1)], w_send.at[1])
+    for half in range(2):
+        wait_bytes(w_full.at[blocks[half], 0, 0, pl.ds(0, 3)], w_send.at[1 + half])
+        wait_bytes(w_full.at[blocks[half], 0, pl.ds(0, 3)], w_send.at[3 + half])
     w_half.wait_send()
     wait_bytes(mix.at[pl.ds(0, TP - 1)], mix_send)
 
@@ -461,7 +471,7 @@
         pltpu.VMEM((CHIPS, OWN, CHUNK), BF16),
         pltpu.VMEM((4, 4, TP * WIDTH), BF16),
         pltpu.VMEM((16, TP * WIDTH), F32),
-        pltpu.VMEM((TP, 2, PLANES, 16, WIDTH), BF16),
+        pltpu.VMEM((TP, 2, 4, 4, 16, WIDTH), BF16),
         pltpu.VMEM((LANES, CHUNK), F32),
         pltpu.VMEM((TP, WIDTH, CHUNK), BF16),
         pltpu.VMEM((WIDTH, CHUNK), F32),
@@ -477,8 +487,8 @@
         dma((4,)),
         dma,
         dma((TILES,)),
-        dma((3,)),
-        dma((3,)),
+        dma((6,)),
+        dma((6,)),
         dma,
         dma((TP,)),
     ]

time: 65.9 us -> 65.8 us (level)
  no operation moved by 1% of the time
where the time goes in v5:
time: 65.8 us; the launch traced here: 65.7 us
  Pallas kernels  65 us (99%)
  local copies, waits for them, and re-layouts  0.66 us (1%)
    pallas_call x1, Pallas kernels, local(): pl.pallas_call(mixer_kernel, out_shape=jax.ShapeDtypeStruct((CHUNK, WIDTH...  65 us

profile of v5, /device:TPU:1, one launch (start us, length us, event | category | flops | bytes accessed | tf_op | source)
XLA Modules:
  0.0 65.7 jit_solution(272149347726541687)
XLA Ops:
  0.0 65.0 %mixer.1 = bf16[128,512]{1,0:T(8,128)(2,1)S(1)} custom-call(bf16[128,512]{1,0:T(8,128)(2,1)} %gate_hbm.1, bf16[128,512]{1,0:T(8,128)(2,1)} %post_hbm.1, bf16[128,512]{1,0:T(8,128)(2,1)} %vals_hbm.1, f32[2,16,512]{2,1,0:T(8,128)} %bitcast.2, f32[2,16,512]{2,1,0:T(8,128)} %bitcast.3, bf16[4,2048]{1,0:T(4,128)(2,1)} %w_hbm.1), custom_call_target="tpu_custom_call" | custom-call | tf_op jit(solution)/shard_map/mixer/pallas_call | solution.py:495
  65.0 0.7 %copy.8 = bf16[128,512]{1,0:T(8,128)(2,1)} copy(bf16[128,512]{1,0:T(8,128)(2,1)S(1)} %mixer.1) | data formatting | bytes 262144

commit v6 on v5

--- a/solution.py
+++ b/solution.py
@@ -151,9 +151,6 @@
             ]
         )
     ]
-    for load in loads:
-        load.start()
-
     barrier = pltpu.get_barrier_semaphore()
     for step in STEPS:
         pl.semaphore_signal(
@@ -162,6 +159,8 @@
     for other in tp_peers:
         pl.semaphore_signal(barrier, inc=1, device_id={"tp": other}, device_id_type=MESH)
     pl.semaphore_signal(barrier, inc=1, device_id=sibling, device_id_type=MESH)
+    for load in loads:
+        load.start()
 
     def spread(source, target):
         for tile in range(TILES):
@@ -401,20 +400,25 @@
             )
         rows = pl.ds(pl.multiple_of(tile * LANES, LANES), LANES)
         mix[tp, rows, :] = mix_f32[...].astype(BF16)
-        for other in reversed(tp_peers):
-            remote(
-                mix.at[tp, rows], mix.at[tp, rows], mix_send, mix_recv.at[tp], {"tp": other}
-            ).start()
-
-    w_half.wait_recv()
+        part = mix.at[tp, rows]
+        remote(part, part, mix_send, mix_recv.at[2 + tile], {"tp": tp_peers[1]}).start()
+        remote(part, part, mix_send, mix_recv.at[0], {"tp": tp_peers[0]}).start()
 
     def project(block):
         return matmul(w_full[block].reshape(WIDTH, WIDTH), mix[block])
 
+    w_half.wait_recv()
     acc[...] = project(tp)
-    for block in tp_peers:
-        wait_bytes(mix.at[block], mix_recv.at[block])
-        acc[...] += project(block)
+    for offset in range(TILES):
+        tile = lax.rem(x_pos + offset, TILES)
+        part = mix.at[tp_peers[1], pl.ds(pl.multiple_of(tile * LANES, LANES), LANES)]
+        wait_bytes(part, mix_recv.at[2 + tile])
+        remote(part, part, mix_send, mix_recv.at[1], {"tp": tp_peers[0]}).start()
+    acc[...] += project(tp_peers[1])
+    wait_bytes(mix.at[tp_peers[0]], mix_recv.at[0])
+    acc[...] += project(tp_peers[0])
+    wait_bytes(mix.at[tp_peers[2]], mix_recv.at[1])
+    acc[...] += project(tp_peers[2])
     for group in range(CHIPS):
         for part in range(2):
             first = part * (WIDTH // 2) + group * 4
@@ -490,7 +494,7 @@
         dma((6,)),
         dma((6,)),
         dma,
-        dma((TP,)),
+        dma((2 + TILES,)),
     ]
     return pl.pallas_call(
         mixer_kernel,

time: 65.8 us -> 64.3 us (0.977)
  Pallas kernels: 65 us -> 63.5 us
    pallas_call x1, Pallas kernels: 65 us -> 63.5 us  [local(): pl.pallas_call(mixer_kernel, out_shape=jax.ShapeDtypeStruct((CHUNK, WIDTH...]
where the time goes in v6:
time: 64.3 us; the launch traced here: 64.2 us
  Pallas kernels  63.5 us (99%)
  local copies, waits for them, and re-layouts  0.66 us (1%)
    pallas_call x1, Pallas kernels, local(): pl.pallas_call(mixer_kernel, out_shape=jax.ShapeDtypeStruct((CHUNK, WIDTH...  63.5 us

profile of v6, /device:TPU:1, one launch (start us, length us, event | category | flops | bytes accessed | tf_op | source)
XLA Modules:
  0.0 64.2 jit_solution(6218982824585296807)
XLA Ops:
  0.0 63.5 %mixer.1 = bf16[128,512]{1,0:T(8,128)(2,1)S(1)} custom-call(bf16[128,512]{1,0:T(8,128)(2,1)} %gate_hbm.1, bf16[128,512]{1,0:T(8,128)(2,1)} %post_hbm.1, bf16[128,512]{1,0:T(8,128)(2,1)} %vals_hbm.1, f32[2,16,512]{2,1,0:T(8,128)} %bitcast.2, f32[2,16,512]{2,1,0:T(8,128)} %bitcast.3, bf16[4,2048]{1,0:T(4,128)(2,1)} %w_hbm.1), custom_call_target="tpu_custom_call" | custom-call | tf_op jit(solution)/shard_map/mixer/pallas_call | solution.py:499
  63.5 0.7 %copy.8 = bf16[128,512]{1,0:T(8,128)(2,1)} copy(bf16[128,512]{1,0:T(8,128)(2,1)S(1)} %mixer.1) | data formatting | bytes 262144

commit v7 on v6

--- a/solution.py
+++ b/solution.py
@@ -209,15 +209,16 @@
         remote(v_out.at[other], v_in.at[chip, core], v_send, v_recv, same_core(other)).start()
     v_in[chip, core] = v_out[chip]
 
+    for step in STEPS:
+        other = moved(step)
+        remote(g_out.at[other], g_in.at[chip, core], g_send, g_recv, same_core(other)).start()
+    g_in[chip, core] = g_out[chip]
+
     for offset in (2, 1, 3):
         other = plane * 4 + lax.rem(z_hi + offset, 4)
         remote(
             w_planes.at[z_hi], w_planes.at[z_hi], w_send.at[0], w_recv.at[0], same_core(other)
         ).start()
-    for step in STEPS:
-        other = moved(step)
-        remote(g_out.at[other], g_in.at[chip, core], g_send, g_recv, same_core(other)).start()
-    g_in[chip, core] = g_out[chip]
 
     par_copy.wait_recv()
     poles = jnp.where(core == 1, par_in[...], par_own[...])
@@ -297,6 +298,33 @@
             value = value + jnp.exp(-float(CHUNK * count) * decay) * later(value, count)
         return value
 
+    wait_bytes(v_in.at[pl.ds(0, CHIPS - 1), 0], v_recv)
+    v_near = near(v_in, 0)
+    v_near.start()
+    v_near.wait_recv()
+    gather_rows(v_in, v_rows)
+
+    states = jnp.zeros(square, F32)
+    for channel in range(OWN):
+        line = picked(v_rows, channel).astype(BF16)
+        both = matmul(line, table_high[0, channel]) + matmul(line, table_low[0, channel])
+        y_rows[channel] = both[:, :LANES]
+        states = states + both[:, LANES:]
+    carry = scan(states, 0)
+    wait_bytes(g_in.at[pl.ds(0, CHIPS - 1), 0], g_recv)
+    g_near = near(g_in, 1)
+    g_near.start()
+
+    g_near.wait_recv()
+    gather_rows(g_in, g_rows)
+
+    states = jnp.zeros(square, F32)
+    for channel in range(OWN):
+        value = y_rows[channel] + product3(carry, back_high[0, channel], back_low[0, channel])
+        value = value * picked(g_rows, channel)
+        both = product3(value, table_high[1, channel], table_low[1, channel])
+        y_rows[channel] = both[:, :LANES]
+        states = states + both[:, LANES:]
     wait_bytes(w_planes.at[pl.ds(0, 3)], w_recv.at[0])
     for other in range(4):
         w_block[other * 4 : other * 4 + 4, :] = w_planes[other].astype(F32)
@@ -316,36 +344,6 @@
     along(1, w_full.at[blocks[0], core, x_pos, y_pos], 1)
     along(0, w_full.at[blocks[1], core, x_pos, y_pos], 2)
 
-    wait_bytes(v_in.at[pl.ds(0, CHIPS - 1), 0], v_recv)
-    v_near = near(v_in, 0)
-    v_near.start()
-    v_near.wait_recv()
-    gather_rows(v_in, v_rows)
-
-    states = jnp.zeros(square, F32)
-    for channel in range(OWN):
-        line = picked(v_rows, channel).astype(BF16)
-        both = matmul(line, table_high[0, channel]) + matmul(line, table_low[0, channel])
-        y_rows[channel] = both[:, :LANES]
-        states = states + both[:, LANES:]
-    carry = scan(states, 0)
-    for half in range(2):
-        wait_bytes(w_full.at[blocks[half], 0, 0, pl.ds(0, 3)], w_recv.at[1 + half])
-    along(0, w_full.at[blocks[0], core, x_pos], 3)
-    along(1, w_full.at[blocks[1], core, :, y_pos], 4)
-    wait_bytes(g_in.at[pl.ds(0, CHIPS - 1), 0], g_recv)
-    g_near = near(g_in, 1)
-    g_near.start()
-    g_near.wait_recv()
-    gather_rows(g_in, g_rows)
-
-    states = jnp.zeros(square, F32)
-    for channel in range(OWN):
-        value = y_rows[channel] + product3(carry, back_high[0, channel], back_low[0, channel])
-        value = value * picked(g_rows, channel)
-        both = product3(value, table_high[1, channel], table_low[1, channel])
-        y_rows[channel] = both[:, :LANES]
-        states = states + both[:, LANES:]
     carry = scan(states, 1)
 
     y_near = []
@@ -385,10 +383,9 @@
     y_in[chip] = y_out[chip]
 
     for half in range(2):
-        wait_bytes(w_full.at[blocks[half], 0, pl.ds(0, 3)], w_recv.at[3 + half])
-    part = w_full.at[:, core]
-    w_half = remote(part, part, w_send.at[5], w_recv.at[5], sibling)
-    w_half.start()
+        wait_bytes(w_full.at[blocks[half], 0, 0, pl.ds(0, 3)], w_recv.at[1 + half])
+    along(0, w_full.at[blocks[0], core, x_pos], 3)
+    along(1, w_full.at[blocks[1], core, :, y_pos], 4)
 
     for offset in range(TILES):
         tile = lax.rem(x_pos + offset, TILES)
@@ -403,6 +400,12 @@
         part = mix.at[tp, rows]
         remote(part, part, mix_send, mix_recv.at[2 + tile], {"tp": tp_peers[1]}).start()
         remote(part, part, mix_send, mix_recv.at[0], {"tp": tp_peers[0]}).start()
+
+    for half in range(2):
+        wait_bytes(w_full.at[blocks[half], 0, pl.ds(0, 3)], w_recv.at[3 + half])
+    part = w_full.at[:, core]
+    w_half = remote(part, part, w_send.at[5], w_recv.at[5], sibling)
+    w_half.start()
 
     def project(block):
         return matmul(w_full[block].reshape(WIDTH, WIDTH), mix[block])

time: 64.3 us -> 63.4 us (0.986)
  Pallas kernels: 63.5 us -> 62.6 us
    pallas_call x1, Pallas kernels: 63.5 us -> 62.6 us  [local(): pl.pallas_call(mixer_kernel, out_shape=jax.ShapeDtypeStruct((CHUNK, WIDTH...]
where the time goes in v7:
time: 63.4 us; the launch traced here: 63.3 us
  Pallas kernels  62.6 us (99%)
  local copies, waits for them, and re-layouts  0.66 us (1%)
    pallas_call x1, Pallas kernels, local(): pl.pallas_call(mixer_kernel, out_shape=jax.ShapeDtypeStruct((CHUNK, WIDTH...  62.6 us

profile of v7, /device:TPU:1, one launch (start us, length us, event | category | flops | bytes accessed | tf_op | source)
XLA Modules:
  0.0 63.3 jit_solution(8194519316420591059)
XLA Ops:
  0.0 62.6 %mixer.1 = bf16[128,512]{1,0:T(8,128)(2,1)S(1)} custom-call(bf16[128,512]{1,0:T(8,128)(2,1)} %gate_hbm.1, bf16[128,512]{1,0:T(8,128)(2,1)} %post_hbm.1, bf16[128,512]{1,0:T(8,128)(2,1)} %vals_hbm.1, f32[2,16,512]{2,1,0:T(8,128)} %bitcast.2, f32[2,16,512]{2,1,0:T(8,128)} %bitcast.3, bf16[4,2048]{1,0:T(4,128)(2,1)} %w_hbm.1), custom_call_target="tpu_custom_call" | custom-call | tf_op jit(solution)/shard_map/mixer/pallas_call | solution.py:502
  62.6 0.7 %copy.8 = bf16[128,512]{1,0:T(8,128)(2,1)} copy(bf16[128,512]{1,0:T(8,128)(2,1)S(1)} %mixer.1) | data formatting | bytes 262144

commit v8 on v7

--- a/solution.py
+++ b/solution.py
@@ -358,7 +358,8 @@
             )
             o_rows[pl.ds(half * CHIPS * OWN + channel, CHIPS, stride=OWN), :] = value
         for part in parts:
-            y_give[part] = o_rows[(2 * part + 1) * OWN : (2 * part + 2) * OWN, :]
+            given = o_rows[(2 * part + 1) * OWN : (2 * part + 2) * OWN, :]
+            y_give[part] = given.astype(BF16)
         piece = pl.ds(half * CHIPS // 2, CHIPS // 2)
         copy = remote(
             y_give.at[piece],
@@ -373,7 +374,8 @@
         y_near[1 - half].wait_recv()
         for part in range(half * CHIPS // 2, (half + 1) * CHIPS // 2):
             place = part + core * (CHIPS - 1 - 2 * part)
-            total = o_rows[2 * part * OWN : (2 * part + 1) * OWN, :] + y_take[CHIPS - 1 - part]
+            kept = o_rows[2 * part * OWN : (2 * part + 1) * OWN, :]
+            total = kept + y_take[CHIPS - 1 - part].astype(F32)
             y_out[place] = total.astype(BF16)
     for step in STEPS:
         other = moved(step)
@@ -387,7 +389,7 @@
     along(0, w_full.at[blocks[0], core, x_pos], 3)
     along(1, w_full.at[blocks[1], core, :, y_pos], 4)
 
-    for offset in range(TILES):
+    for offset in (0, 1, 3, 2):
         tile = lax.rem(x_pos + offset, TILES)
         wait_bytes(y_in.at[pl.ds(0, 15 if offset == 0 else 16)], out_recv.at[tile])
         for part in range(16):
@@ -412,7 +414,7 @@
 
     w_half.wait_recv()
     acc[...] = project(tp)
-    for offset in range(TILES):
+    for offset in (0, 1, 3, 2):
         tile = lax.rem(x_pos + offset, TILES)
         part = mix.at[tp_peers[1], pl.ds(pl.multiple_of(tile * LANES, LANES), LANES)]
         wait_bytes(part, mix_recv.at[2 + tile])
@@ -472,8 +474,8 @@
         pltpu.VMEM((2, 8, LANES), F32),
         pltpu.VMEM((OWN, CHUNKS, CHUNK), F32),
         pltpu.VMEM((CHUNKS * OWN, CHUNK), F32),
-        pltpu.VMEM((CHIPS, OWN, CHUNK), F32),
-        pltpu.VMEM((CHIPS, OWN, CHUNK), F32),
+        pltpu.VMEM((CHIPS, OWN, CHUNK), BF16),
+        pltpu.VMEM((CHIPS, OWN, CHUNK), BF16),
         pltpu.VMEM((CHIPS, OWN, CHUNK), BF16),
         pltpu.VMEM((CHIPS, OWN, CHUNK), BF16),
         pltpu.VMEM((4, 4, TP * WIDTH), BF16),

time: 63.4 us -> 63.6 us (level)
  no operation moved by 1% of the time
where the time goes in v8:
time: 63.6 us; the launch traced here: 63.4 us
  Pallas kernels  62.8 us (99%)
  local copies, waits for them, and re-layouts  0.66 us (1%)
    pallas_call x1, Pallas kernels, local(): pl.pallas_call(mixer_kernel, out_shape=jax.ShapeDtypeStruct((CHUNK, WIDTH...  62.8 us

profile of v8, /device:TPU:1, one launch (start us, length us, event | category | flops | bytes accessed | tf_op | source)
XLA Modules:
  0.0 63.4 jit_solution(16396933401818815369)
XLA Ops:
  0.0 62.8 %mixer.1 = bf16[128,512]{1,0:T(8,128)(2,1)S(1)} custom-call(bf16[128,512]{1,0:T(8,128)(2,1)} %gate_hbm.1, bf16[128,512]{1,0:T(8,128)(2,1)} %post_hbm.1, bf16[128,512]{1,0:T(8,128)(2,1)} %vals_hbm.1, f32[2,16,512]{2,1,0:T(8,128)} %bitcast.2, f32[2,16,512]{2,1,0:T(8,128)} %bitcast.3, bf16[4,2048]{1,0:T(4,128)(2,1)} %w_hbm.1), custom_call_target="tpu_custom_call" | custom-call | tf_op jit(solution)/shard_map/mixer/pallas_call | solution.py:504
  62.8 0.7 %copy.8 = bf16[128,512]{1,0:T(8,128)(2,1)} copy(bf16[128,512]{1,0:T(8,128)(2,1)S(1)} %mixer.1) | data formatting | bytes 262144

commit v9 on v7

--- a/solution.py
+++ b/solution.py
@@ -410,13 +410,13 @@
     def project(block):
         return matmul(w_full[block].reshape(WIDTH, WIDTH), mix[block])
 
-    w_half.wait_recv()
-    acc[...] = project(tp)
     for offset in range(TILES):
         tile = lax.rem(x_pos + offset, TILES)
         part = mix.at[tp_peers[1], pl.ds(pl.multiple_of(tile * LANES, LANES), LANES)]
         wait_bytes(part, mix_recv.at[2 + tile])
         remote(part, part, mix_send, mix_recv.at[1], {"tp": tp_peers[0]}).start()
+    w_half.wait_recv()
+    acc[...] = project(tp)
     acc[...] += project(tp_peers[1])
     wait_bytes(mix.at[tp_peers[0]], mix_recv.at[0])
     acc[...] += project(tp_peers[0])

time: 63.4 us -> 62.6 us (0.987)
  Pallas kernels: 62.6 us -> 61.8 us
    pallas_call x1, Pallas kernels: 62.6 us -> 61.8 us  [local(): pl.pallas_call(mixer_kernel, out_shape=jax.ShapeDtypeStruct((CHUNK, WIDTH...]
where the time goes in v9:
time: 62.6 us; the launch traced here: 62.4 us
  Pallas kernels  61.8 us (99%)
  local copies, waits for them, and re-layouts  0.66 us (1%)
    pallas_call x1, Pallas kernels, local(): pl.pallas_call(mixer_kernel, out_shape=jax.ShapeDtypeStruct((CHUNK, WIDTH...  61.8 us

profile of v9, /device:TPU:1, one launch (start us, length us, event | category | flops | bytes accessed | tf_op | source)
XLA Modules:
  0.0 62.4 jit_solution(17208817707835285446)
XLA Ops:
  0.0 61.8 %mixer.1 = bf16[128,512]{1,0:T(8,128)(2,1)S(1)} custom-call(bf16[128,512]{1,0:T(8,128)(2,1)} %gate_hbm.1, bf16[128,512]{1,0:T(8,128)(2,1)} %post_hbm.1, bf16[128,512]{1,0:T(8,128)(2,1)} %vals_hbm.1, f32[2,16,512]{2,1,0:T(8,128)} %bitcast.2, f32[2,16,512]{2,1,0:T(8,128)} %bitcast.3, bf16[4,2048]{1,0:T(4,128)(2,1)} %w_hbm.1), custom_call_target="tpu_custom_call" | custom-call | tf_op jit(solution)/shard_map/mixer/pallas_call | solution.py:502
  61.8 0.7 %copy.8 = bf16[128,512]{1,0:T(8,128)(2,1)} copy(bf16[128,512]{1,0:T(8,128)(2,1)S(1)} %mixer.1) | data formatting | bytes 262144
